TPU v7x, 256 devices: a whole 4x4x8 slice. The times are simulated.
256 devices in a mesh: cube: 4 (over y), row: 4 (over x), col: 16 (over z, core).
Axes of the slice: x: 4, y: 4, z: 8, core: 2. Of those that a mesh axis runs over, the one named last changes fastest.
Arguments:
- front_entries: float32 [4, 8192, 8192], P('cube', 'row', 'col'), as said below
- child_updates: float32 [4, 2, 4096, 4096], P('cube', None, ('row', 'col')), may hold values from -6 to 6, as said below
- child_index: int32 [4, 2, 64], replicated, may hold values from 0 to 127, as said below
- child_blocks: int32 [4, 2], replicated, may hold values from 32 to 64
Outputs:
- factored: float32 [4, 8192, 8192], P('cube', 'row', 'col')
Inputs may be any that keep to these rules, and one draw needn't show every extreme that they name: `front_entries`: each front is symmetric positive definite in natural numbering. `child_updates`: each contribution block is symmetric. `child_index`: each list names 64 different front blocks; entry t of a list names a front block whose rows lie in a 512-wide block b of front variables with b mod 4 = t div (16).
All inputs are finite; a program needn't handle non-finite values.
Results may differ from a plain program's by a relative error of at most 0.0001.
Values sent between devices are 32-bit elements; how exact they have to be, the bound alone decides.
No kernel may reach another device: no remote copies, remote signals or barrier semaphores. Data moves between devices by JAX's collectives and lax.ppermute only.
A program may use at most 128 MiB of HBM per device.

v0:
```python
import jax
import jax.numpy as jnp
from jax import lax
from jax.sharding import PartitionSpec as P

F = 8192
B = 512
SBLK = 64
CR = 4096
PANELS = 2


HIGHEST_PRECISION = lax.Precision.HIGHEST


def swapped(value, axis, apart):
    mask = 2**apart
    pairs = [(source, source ^ mask) for source in range(lax.axis_size(axis))]
    return lax.ppermute(value, axis, pairs)


def spread_2(block, axis, holder):
    block = jnp.where(lax.axis_index(axis) == holder, block, jnp.zeros_like(block))
    return lax.psum(block, axis)


def storage_position(variable, parts, local_size):
    block = variable // B
    return block % parts * local_size + block // parts * B + variable % B


def natural_variable(local_size, parts, index):
    local = jnp.arange(local_size, dtype=jnp.int32)
    return (local // B * parts + index) * B + local % B


def child_variable(block_lists, offsets):
    return jnp.take(block_lists, offsets // SBLK, axis=1) * SBLK + offsets % SBLK


def solve_panel(rows_in, factor, row_block, panel_step, row_index, root_row, row_slot):
    solved = lax.linalg.triangular_solve(
        factor, rows_in, left_side=False, lower=True, transpose_a=True
    )
    solved = jnp.where((row_block < panel_step)[:, None], 0.0, solved)
    with_pivot = lax.dynamic_update_slice(solved, factor, (row_slot * B, 0))
    return jnp.where(row_index == root_row, with_pivot, solved)


def on_device(front_entries, child_updates, child_index, child_blocks):
    n_row = lax.axis_size("row")
    n_col = lax.axis_size("col")
    row_index = lax.axis_index("row")
    col_index = lax.axis_index("col")
    cube_index = lax.axis_index("cube")
    sibling = jnp.bitwise_xor(cube_index, 1)
    working = front_entries[0]
    rows_here, cols_here = working.shape
    piece_rows = child_updates.shape[2]
    arrived_child = swapped(child_updates[0, 1], "cube", 0)
    pieces = jnp.stack([child_updates[0, 0], arrived_child])
    block_lists = jnp.stack([child_index[cube_index, 0], child_index[sibling, 1]])
    counts = jnp.stack([child_blocks[cube_index, 0], child_blocks[sibling, 1]])
    offsets = jnp.arange(CR, dtype=jnp.int32)
    flat_index = row_index * n_col + col_index
    own_rows = flat_index * piece_rows + jnp.arange(piece_rows, dtype=jnp.int32)
    live_cols = (offsets // SBLK)[None, :] < counts[:, None]
    live_rows = (own_rows // SBLK)[None, :] < counts[:, None]
    values = jnp.where(live_rows[:, :, None] & live_cols[:, None, :], pieces, 0.0)
    col_targets = storage_position(child_variable(block_lists, offsets), n_col, cols_here)

    def widen(child_values, targets):
        return jnp.zeros((piece_rows, F), jnp.float32).at[:, targets].add(child_values)

    spread = jax.vmap(widen)(values, col_targets).reshape(2 * piece_rows, F)
    arrived = lax.all_to_all(spread, "col", split_axis=1, concat_axis=0, tiled=True)
    sources = jnp.arange(n_col, dtype=jnp.int32)
    source_rows = (row_index * n_col + sources)[:, None] * piece_rows + jnp.arange(
        piece_rows, dtype=jnp.int32
    )[None, :]
    natural_rows = child_variable(block_lists, source_rows)
    row_targets = storage_position(jnp.swapaxes(natural_rows, 0, 1), n_row, rows_here).reshape(-1)
    local_rows = row_targets - row_index * rows_here
    working = working.at[local_rows].add(arrived)
    row_block = natural_variable(rows_here, n_row, row_index) // B
    col_block = natural_variable(cols_here, n_col, col_index) // B
    identity = jnp.eye(B, dtype=jnp.float32)
    for panel_step in range(PANELS):
        root_row = panel_step % n_row
        row_slot = panel_step // n_row
        root_col = panel_step % n_col
        col_slot = panel_step // n_col
        diagonal = working[row_slot * B : (row_slot + 1) * B, col_slot * B : (col_slot + 1) * B]
        panel_cols = working
        own_pivot = jnp.where(col_index == root_col, diagonal, identity)
        pivot_block = spread_2(own_pivot, "row", root_row)
        factor = jnp.linalg.cholesky(pivot_block)
        own_lower = solve_panel(
            panel_cols, factor, row_block, panel_step, row_index, root_row, row_slot
        )
        lower_rows = spread_2(own_lower, "col", root_col)
        global_block = 0 + col_index
        block_piece = lax.dynamic_slice_in_dim(lower_rows, global_block // n_row * B, B, 0)
        col_pieces = jnp.where(global_block % n_row == row_index, block_piece, 0.0)
        lower_cols = lax.psum(col_pieces, "row")
        working = working - jnp.dot(
            lower_rows,
            lower_cols.T,
            precision=HIGHEST_PRECISION,
            preferred_element_type=jnp.float32,
        )
        replaced = working.at[:, col_slot * B : (col_slot + 1) * B].set(lower_rows)
        working = jnp.where(col_index == root_col, replaced, working)
    finished = (row_block < PANELS)[:, None] & (col_block >= PANELS)[None, :]
    return jnp.where(finished, 0.0, working)[None]


def solution(mesh):
    in_specs = (P("cube", "row", "col"), P("cube", None, ("row", "col"), None), P(), P())
    out_specs = P("cube", "row", "col")
    return jax.shard_map(
        on_device, mesh=mesh, in_specs=in_specs, out_specs=out_specs, check_vma=False
    )
```

profile of v0, /device:TPU:97, one launch (start us, length us, event | category | flops | bytes accessed | tf_op | source)
XLA Modules:
  0.0 1047.8 jit_solution(9398155492795176346)
XLA Ops:
  6.5 4.8 copy.227
  15.3 14.1 %gather_fusion.1 = s32[4096,2]{1,0:T(8,128)} fusion(s32[2,64]{0,1:T(8,128)S(1)} %copy.127, s32[4096]{0:T(1024)S(1)} %broadcast_clamp_fusion), kind=kCustom, calls=%fused_computation.1 | custom fusion | bytes 81920 | tf_op jit(solution)/shard_map/jit(_take)/gather | solution.py:38
  29.4 7.2 compare_select_fusion
  41.1 2.6 broadcast_select_fusion.2
  47.6 2.7 copy.174
  50.4 48.2 %scatter_custom_fusion.1 = f32[16384,64]{1,0:T(8,128)} fusion(s32[8192]{0:T(1024)S(1)} %bitcast.172, f32[8192,64]{1,0:T(8,128)} %bitcast.167, f32[]{:T(128)} %constant.447.clone.1), kind=kCustom, calls=%fused_computation.11 | custom fusion | flops 524288 | bytes 4194816
  98.6 8.7 copy.175
  107.3 4.6 copy.137
  111.9 3.3 copy.182
  115.1 4.4 copy.138
  119.5 8.3 all-to-all-start
  128.0 2.8 gather_fusion
  131.5 90.0 %all-to-all-done = f32[128,16,512]{2,0,1:T(8,128)} async-done(((f32[128,16,512]{2,0,1:T(8,128)}), f32[128,16,512]{2,0,1:T(8,128)}, u32[]{:S(2)}, u32[]{:S(2)}) %all-to-all-start) | async-done | bytes 4194336 | tf_op jit(solution)/shard_map/all_to_all | solution.py:76
  221.5 17.4 %scatter_fusion = f32[2048,512]{1,0:T(8,128)} fusion(f32[2048,512]{1,0:T(8,128)} %bitcast.156, s32[2048]{0:T(1024)S(1)} %bitcast.171, f32[2048,512]{1,0:T(8,128)} %bitcast.19), kind=kCustom, calls=%fused_computation.2 | custom fusion | flops 1048576 | bytes 12591104 | tf_op jit(solution)/shard_map/scatter-add | solution.py:84
  238.9 5.4 copy.139
  247.2 48.2 %all-reduce.8.cloned.1.call-done = f32[512,512]{0,1:T(8,128)} async-done(((f32[512,512]{0,1:T(8,128)}), f32[512,512]{0,1:T(8,128)}) %all-reduce.8.cloned.1.call-update) | async-done | bytes 1048592 | tf_op jit(solution)/shard_map/psum | solution.py:24
  298.4 11.7 %cholesky.286 = f32[128,128]{1,0:T(8,128)S(1)} custom-call(f32[128,128]{1,0:T(8,128)S(1)} %cholesky.426), custom_call_target="Cholesky" | custom-call | tf_op jit(solution)/shard_map/jit(cholesky)/cholesky | solution.py:97
  310.2 9.8 custom-call.27
  320.7 11.7 %cholesky.305 = f32[128,128]{1,0:T(8,128)S(1)} custom-call(f32[128,128]{1,0:T(8,128)S(1)} %cholesky.430), custom_call_target="Cholesky" | custom-call | tf_op jit(solution)/shard_map/jit(cholesky)/cholesky | solution.py:97
  332.7 9.9 custom-call.28
  343.8 11.7 %cholesky.326 = f32[128,128]{1,0:T(8,128)S(1)} custom-call(f32[128,128]{1,0:T(8,128)S(1)} %cholesky.435), custom_call_target="Cholesky" | custom-call | tf_op jit(solution)/shard_map/jit(cholesky)/cholesky | solution.py:97
  355.7 9.8 custom-call.29
  366.3 11.9 %cholesky.343 = f32[128,128]{1,0:T(8,128)S(1)} custom-call(f32[128,128]{1,0:T(8,128)S(1)} %convolution_subtract_fusion.9), custom_call_target="Cholesky" | custom-call | tf_op jit(solution)/shard_map/jit(cholesky)/cholesky | solution.py:97
  383.0 8.3 while.8
  391.3 39.3 %custom-call.30 = f32[4,128,128]{1,2,0:T(8,128)S(1)} custom-call(f32[4,128,128]{2,1,0:T(8,128)S(1)} %get-tuple-element.61), custom_call_target="InvertDiagBlocksLowerTriangular" | custom-call | tf_op jit(solution)/shard_map/triangular_solve/custom-call.3 | solution.py:42
  430.6 2.4 fusion.44
  433.1 3.0 convolution_subtract_fusion.3
  437.2 3.5 convolution_subtract_fusion.1
  441.7 5.6 fusion.17
  449.3 2.6 broadcast_select_fusion.1
  452.0 123.9 %all-reduce.10.cloned.1.call-done = f32[2048,512]{0,1:T(8,128)} async-done(((f32[2048,512]{0,1:T(8,128)}), f32[2048,512]{0,1:T(8,128)}) %all-reduce.10.cloned.1.call-update) | async-done | bytes 4194320 | tf_op jit(solution)/shard_map/psum | solution.py:24
  578.3 49.6 %all-reduce.12.cloned.1.call-done = f32[512,512]{0,1:T(8,128)} async-done(((f32[512,512]{0,1:T(8,128)}), f32[512,512]{0,1:T(8,128)}) %all-reduce.12.cloned.1.call-update) | async-done | bytes 1048592 | tf_op jit(solution)/shard_map/psum | solution.py:105
  627.8 11.9 %subtract_select_fusion = f32[2048,512]{0,1:T(8,128)S(1)} fusion(f32[2048,512]{0,1:T(8,128)} %all-reduce.10.cloned.1.call-done, f32[2048,512]{0,1:T(8,128)} %copy.139, f32[512,512]{0,1:T(8,128)} %all-reduce.12.cloned.1.call-done, pred[]{:T(512)S(6)} %eq.46), kind=kOutput, calls=%fused_computation.14 | convolution fusion | flops 6444548096 | bytes 13631489 | tf_op jit(solution)/shard_map/dot_general | solution.py:106
  643.2 51.7 %all-reduce.14.cloned.1.call-done = f32[512,512]{0,1:T(8,128)} async-done(((f32[512,512]{0,1:T(8,128)}), f32[512,512]{0,1:T(8,128)}) %all-reduce.14.cloned.1.call-update) | async-done | bytes 1048592 | tf_op jit(solution)/shard_map/psum | solution.py:24
  697.9 11.7 %cholesky.358 = f32[128,128]{1,0:T(8,128)S(1)} custom-call(f32[128,128]{1,0:T(8,128)S(1)} %cholesky.439), custom_call_target="Cholesky" | custom-call | tf_op jit(solution)/shard_map/jit(cholesky)/cholesky | solution.py:97
  709.7 9.8 custom-call.31
  720.1 11.7 %cholesky.377 = f32[128,128]{1,0:T(8,128)S(1)} custom-call(f32[128,128]{1,0:T(8,128)S(1)} %cholesky.443), custom_call_target="Cholesky" | custom-call | tf_op jit(solution)/shard_map/jit(cholesky)/cholesky | solution.py:97
  732.2 10.2 custom-call.32
  743.5 11.7 %cholesky.398 = f32[128,128]{1,0:T(8,128)S(1)} custom-call(f32[128,128]{1,0:T(8,128)S(1)} %cholesky.448), custom_call_target="Cholesky" | custom-call | tf_op jit(solution)/shard_map/jit(cholesky)/cholesky | solution.py:97
  755.4 9.8 custom-call.33
  766.0 11.9 %cholesky.415 = f32[128,128]{1,0:T(8,128)S(1)} custom-call(f32[128,128]{1,0:T(8,128)S(1)} %convolution_subtract_fusion.8), custom_call_target="Cholesky" | custom-call | tf_op jit(solution)/shard_map/jit(cholesky)/cholesky | solution.py:97
  783.4 8.6 while.9
  792.0 39.3 %custom-call.34 = f32[4,128,128]{1,2,0:T(8,128)S(1)} custom-call(f32[4,128,128]{2,1,0:T(8,128)S(1)} %get-tuple-element.62), custom_call_target="InvertDiagBlocksLowerTriangular" | custom-call | tf_op jit(solution)/shard_map/triangular_solve/custom-call.3 | solution.py:42
  843.8 2.5 broadcast_select_fusion
  846.4 123.8 %all-reduce.16.cloned.1.call-done = f32[2048,512]{0,1:T(8,128)} async-done(((f32[2048,512]{0,1:T(8,128)}), f32[2048,512]{0,1:T(8,128)}) %all-reduce.16.cloned.1.call-update) | async-done | bytes 4194320 | tf_op jit(solution)/shard_map/psum | solution.py:24
  972.6 49.5 %all-reduce.18.cloned.1.call-done = f32[512,512]{0,1:T(8,128)} async-done(((f32[512,512]{0,1:T(8,128)}), f32[512,512]{0,1:T(8,128)}) %all-reduce.18.cloned.1.call-update) | async-done | bytes 1048592 | tf_op jit(solution)/shard_map/psum | solution.py:105
  1022.1 13.3 %select_bitcast_fusion = f32[1,2048,512]{1,2,0:T(8,128)} fusion(f32[2048,512]{0,1:T(8,128)} %all-reduce.16.cloned.1.call-done, f32[2048,512]{0,1:T(8,128)} %copy-done.1, f32[512,512]{0,1:T(8,128)} %all-reduce.18.cloned.1.call-done, pred[]{:T(512)S(6)} %eq.44, pred[2048]{0:T(1024)(128)(4,1)S(1)} %broadcast_compare_fusion.1, pred[512]{0:T(512)(128)(4,1)S(1)} %fusion.135), kind=kOutput, calls=%fused_computation.13 | convolution fusion | flops 6446645248 | bytes 13634049 | tf_op jit(solution)/shard_map/dot_general | solution.py:106
  1035.4 5.3 copy.164
  (186 shorter events, 74.7 us)
Async XLA Ops:
  6.5 4.8 copy-start.3
  11.3 2.5 copy-start.4
  12.5 24.8 %copy-start.6 = (s32[2]{0:T(128)S(1)}, s32[2]{0:T(128)}, u32[]{:S(2)}) copy-start(s32[2]{0:T(128)} %constant.461) | copy-start | bytes 28
  12.5 33.6 %collective-permute-start = (f32[64,4096]{1,0:T(8,128)}, f32[64,4096]{1,0:T(8,128)}, u32[]{:S(2)}, u32[]{:S(2)}) collective-permute-start(f32[64,4096]{1,0:T(8,128)} %get-tuple-element.124), channel_id=1, source_target_pairs={{0,64},{64,0},{128,192},{192,128},{1,65},{65,1},{129,193},{193,129... | collective-permute-start | bytes 3145736 | tf_op jit(solution)/shard_map/ppermute | solution.py:19
  29.4 8.7 copy-start.5
  119.5 102.0 %all-to-all-start = ((f32[128,16,512]{2,0,1:T(8,128)}), f32[128,16,512]{2,0,1:T(8,128)}, u32[]{:S(2)}, u32[]{:S(2)}) async-start(f32[128,16,512]{2,0,1:T(8,128)} %copy.138), calls=%async_computation | async-start | bytes 8388608 | tf_op jit(solution)/shard_map/all_to_all | solution.py:76
  127.8 167.6 %all-reduce.8.cloned.1.call-start = ((), (), s32[]{:S(2)}) async-start(), calls=%async_computation.1 | async-start | bytes 2097152 | tf_op jit(solution)/shard_map/psum | solution.py:24
  246.7 329.2 %all-reduce.10.cloned.1.call-start = ((), (), s32[]{:S(2)}) async-start(), calls=%async_computation.2 | async-start | bytes 8388608 | tf_op jit(solution)/shard_map/psum | solution.py:24
  430.6 6.6 copy-start
  451.9 175.9 %all-reduce.12.cloned.1.call-start = ((), (), s32[]{:S(2)}) async-start(), calls=%async_computation.3 | async-start | bytes 2097152 | tf_op jit(solution)/shard_map/psum | solution.py:105
  578.2 116.7 %all-reduce.14.cloned.1.call-start = ((), (), s32[]{:S(2)}) async-start(), calls=%async_computation.4 | async-start | bytes 2097152 | tf_op jit(solution)/shard_map/psum | solution.py:24
  639.7 2.0 copy-start.1
  642.9 327.3 %all-reduce.16.cloned.1.call-start = ((), (), s32[]{:S(2)}) async-start(), calls=%async_computation.5 | async-start | bytes 8388608 | tf_op jit(solution)/shard_map/psum | solution.py:24
  831.3 5.8 copy-start.2
  846.4 175.8 %all-reduce.18.cloned.1.call-start = ((), (), s32[]{:S(2)}) async-start(), calls=%async_computation.6 | async-start | bytes 2097152 | tf_op jit(solution)/shard_map/psum | solution.py:105
Sparse Core Ops, SparseCore 0:
  246.8 48.5 all-reduce.7
  452.0 123.8 all-reduce.9
  578.4 49.4 all-reduce.11
  643.1 51.7 all-reduce.13
  846.5 123.7 all-reduce.15
  972.7 49.4 all-reduce.17
where the time goes:
time: 1060 us; the launch traced here: 1050 us
  waiting for transfers between devices  537 us (51%)
  other arithmetic  334 us (32%)
  local copies, waits for them, and re-layouts  87.2 us (8%)
  matrix products  59.1 us (6%)
  between operations  19.6 us (2%)
    psum x4, waiting for transfers between devices, spread_2(): return lax.psum(block, axis)  348 us
    another operation x29, other arithmetic, on_device(): factor = jnp.linalg.cholesky(pivot_block)  158 us
    psum x2, waiting for transfers between devices, on_device(): lower_cols = lax.psum(col_pieces, 'row')  99.1 us
    all_to_all x1, waiting for transfers between devices, on_device(): lax.all_to_all(spread, 'col', split_axis=1, concat_axis=0, tiled=True)  90 us
    another operation x5, other arithmetic, solve_panel(): lax.linalg.triangular_solve(factor, rows_in, left_side=False, lower=True,...  78.9 us
    unnamed x4, other arithmetic  51.1 us
    another operation x14, matrix products, solve_panel(): lax.linalg.triangular_solve(factor, rows_in, left_side=False, lower=True,...  29.3 us
    dot_general x2, matrix products, on_device(): jnp.dot(lower_rows, lower_cols.T, precision=HIGHEST_PRECISION, preferred_...  25.2 us
  transfers between devices with their start and end apart: 8, of which 7 were waited for; matrix products, arithmetic and copies ran while one was open for 3% of the time, Pallas kernels for 0%

commit v1 on v0

v1 whole, which is shorter than its diff:
```python
import jax
import jax.numpy as jnp
from jax import lax
from jax.experimental import pallas as pl
from jax.experimental.pallas import tpu as pltpu
from jax.sharding import PartitionSpec as P

F = 8192
B = 512
SBLK = 64
CR = 4096
PANELS = 2
PIVOTS = PANELS * B
PER_PANEL = B // SBLK
TILE = 128
HIGHEST = lax.Precision.HIGHEST
VMEM = pltpu.VMEM
SMEM = pltpu.SMEM


def vmem_spec():
    return pl.BlockSpec(memory_space=VMEM)


def smem_spec():
    return pl.BlockSpec(memory_space=SMEM)


def widen_kernel(list_ref, live_ref, rows_ref, out_ref):
    out_ref[...] = jnp.zeros_like(out_ref)
    lane = lax.broadcasted_iota(jnp.int32, (SBLK, TILE), 1)

    def place(pair, carry):
        both = rows_ref[:, pl.ds(pl.multiple_of(pair * TILE, TILE), TILE)]
        other = pltpu.roll(both, SBLK, 1)
        for half in range(2):
            block = pair * 2 + half
            target = list_ref[block]
            parity = target % 2
            offset = pl.multiple_of(target % PER_PANEL // 2 * TILE, TILE)
            owner = target // PER_PANEL
            moved = jnp.where(parity == half, both, other)
            keep = (lane // SBLK == parity) & (block < live_ref[0])
            spot = (owner, slice(None), pl.ds(offset, TILE))
            out_ref[spot] = jnp.where(keep, moved, out_ref[spot])
        return carry

    lax.fori_loop(0, CR // TILE, place, 0)


def widen(blocks, live, rows):
    return pl.pallas_call(
        widen_kernel,
        out_shape=jax.ShapeDtypeStruct((F // B, SBLK, B), jnp.float32),
        in_specs=[smem_spec(), smem_spec(), vmem_spec()],
        out_specs=vmem_spec(),
        compiler_params=pltpu.CompilerParams(vmem_limit_bytes=16 << 20),
        name="widen",
    )(blocks, live, rows)


def pivot_part_kernel(place_ref, first_ref, second_ref, corner_ref, out_ref):
    out_ref[...] = jnp.zeros_like(out_ref)
    row_index, col_index = place_ref[2], place_ref[3]

    @pl.when((row_index < PANELS) & (col_index < PANELS))
    def _():
        rows = pl.ds(pl.multiple_of(row_index * B, B), B)
        cols = pl.ds(pl.multiple_of(col_index * B, B), B)
        out_ref[rows, cols] = corner_ref[...]

    for child, source in enumerate((first_ref, second_ref)):
        target = place_ref[child]

        @pl.when(target < PANELS * PER_PANEL)
        def _():
            rows = pl.ds(pl.multiple_of(target * SBLK, SBLK), SBLK)
            for panel in range(PANELS):
                cols = slice(panel * B, panel * B + B)
                out_ref[rows, cols] = out_ref[rows, cols] + source[panel]


def pivot_part(place, first, second, corner):
    return pl.pallas_call(
        pivot_part_kernel,
        out_shape=jax.ShapeDtypeStruct((PIVOTS, PIVOTS), jnp.float32),
        in_specs=[smem_spec()] + [vmem_spec()] * 3,
        out_specs=vmem_spec(),
        compiler_params=pltpu.CompilerParams(vmem_limit_bytes=16 << 20),
        name="pivot_part",
    )(place, first, second, corner)


def factor_tile(tile):
    count = TILE // 8
    groups = [tile[8 * g : 8 * g + 8, :] for g in range(count)]
    lane = lax.broadcasted_iota(jnp.int32, (8, TILE), 1)
    sub = lax.broadcasted_iota(jnp.int32, (8, TILE), 0)
    for j in range(TILE):
        g, q = divmod(j, 8)
        at_j = lane == j
        cols = [jnp.broadcast_to(groups[i][:, j : j + 1], (8, TILE)) for i in range(g, count)]
        recip = 1.0 / jnp.broadcast_to(cols[0][q : q + 1, :], (8, TILE))
        row = jnp.broadcast_to(groups[g][q : q + 1, :], (8, TILE)) * recip
        row = jnp.where(at_j, recip, row)
        below = sub > q
        groups[g] = jnp.where(at_j & below, 0.0, groups[g]) - jnp.where(below, cols[0], 0.0) * row
        for i in range(g + 1, count):
            groups[i] = jnp.where(at_j, 0.0, groups[i]) - cols[i - g] * row
    return jnp.concatenate(groups, axis=0)


def inverse_factor_tile(tile):
    out = factor_tile(tile)
    lane = lax.broadcasted_iota(jnp.int32, (TILE, TILE), 1)
    sub = lax.broadcasted_iota(jnp.int32, (TILE, TILE), 0)
    pivots = jnp.sum(jnp.where(lane == sub, out, 0.0), axis=1, keepdims=True)
    root = lax.rsqrt(pivots)
    root = root * (1.5 - 0.5 * pivots * root * root)
    return jnp.where(lane < sub, out, jnp.where(lane == sub, 1.0, 0.0)) * root


def inverse_factor_kernel(square_ref, inv_ref, row_ref):
    inv_ref[...] = square_ref[...]
    lane = lax.broadcasted_iota(jnp.int32, (TILE, TILE), 1)
    sub = lax.broadcasted_iota(jnp.int32, (TILE, TILE), 0)
    identity = jnp.where(lane == sub, 1.0, 0.0)
    steps = PIVOTS // TILE

    def step(k, carry):
        at = pl.ds(pl.multiple_of(k * TILE, TILE), TILE)
        inv_tile = inverse_factor_tile(inv_ref[at, at])
        inv_ref[at, at] = identity
        row_ref[...] = jnp.dot(
            inv_tile, inv_ref[at, :], precision=HIGHEST, preferred_element_type=jnp.float32
        )
        inv_ref[at, :] = row_ref[...]

        def below(i, carry):
            rows = pl.ds(pl.multiple_of(i * TILE, TILE), TILE)
            left = row_ref[:, rows]
            inv_ref[rows, at] = jnp.zeros((TILE, TILE), jnp.float32)
            inv_ref[rows, :] = inv_ref[rows, :] - lax.dot_general(
                left,
                row_ref[...],
                (((0,), (0,)), ((), ())),
                precision=HIGHEST,
                preferred_element_type=jnp.float32,
            )
            return carry

        return lax.fori_loop(k + 1, steps, below, carry)

    lax.fori_loop(0, steps, step, 0)
    for k in range(steps - 1):
        rows = slice(k * TILE, k * TILE + TILE)
        inv_ref[rows, (k + 1) * TILE :] = jnp.zeros((TILE, PIVOTS - (k + 1) * TILE), jnp.float32)


def inverse_factor(square):
    return pl.pallas_call(
        inverse_factor_kernel,
        out_shape=jax.ShapeDtypeStruct((PIVOTS, PIVOTS), jnp.float32),
        in_specs=[vmem_spec()],
        out_specs=vmem_spec(),
        scratch_shapes=[pltpu.VMEM((TILE, PIVOTS), jnp.float32)],
        compiler_params=pltpu.CompilerParams(vmem_limit_bytes=32 << 20),
        name="inverse_factor",
    )(square)


def top_rows_kernel(target_ref, front_ref, first_ref, second_ref, out_ref):
    out_ref[...] = front_ref[...]
    for child, source in enumerate((first_ref, second_ref)):
        for t in range(source.shape[0]):
            target = target_ref[child, t]

            @pl.when(target // (PER_PANEL * 4) == 0)
            def _():
                rows = pl.ds(pl.multiple_of(target % PER_PANEL * SBLK, SBLK), SBLK)
                out_ref[rows, :] = out_ref[rows, :] + source[t]


def top_rows(targets, front, first, second):
    return pl.pallas_call(
        top_rows_kernel,
        grid=(1,),
        out_shape=jax.ShapeDtypeStruct((B, B), jnp.float32),
        in_specs=[
            smem_spec(),
            pl.BlockSpec((B, B), lambda i: (0, 0)),
            vmem_spec(),
            vmem_spec(),
        ],
        out_specs=pl.BlockSpec((B, B), lambda i: (0, 0)),
        compiler_params=pltpu.CompilerParams(vmem_limit_bytes=24 << 20),
        name="top_rows",
    )(targets, front, first, second)


def finish_kernel(
    target_ref, place_ref, front_ref, first_ref, second_ref, base_ref, extra_ref, right_ref,
    out_ref, left_ref,
):
    slot = pl.program_id(0)
    row_index, col_index = place_ref[2], place_ref[3]
    pieces = base_ref.shape[0]
    width = base_ref.shape[2]
    for piece in range(pieces):
        left_ref[:, piece * width : (piece + 1) * width] = base_ref[piece]
    trailing = col_index >= PANELS
    out_ref[...] = jnp.where(trailing, front_ref[...], 0.0)
    for child, source in enumerate((first_ref, second_ref)):
        for t in range(source.shape[0]):
            target = target_ref[child, t]

            @pl.when(target // (PER_PANEL * 4) == slot)
            def _():
                rows = pl.ds(pl.multiple_of(target % PER_PANEL * SBLK, SBLK), SBLK)
                left_ref[rows, :] = left_ref[rows, :] + extra_ref[t, child * SBLK : (child + 1) * SBLK, :]

                @pl.when(trailing)
                def _():
                    out_ref[rows, :] = out_ref[rows, :] + source[t]

    total = out_ref[...] + jnp.dot(
        left_ref[...], right_ref[...], precision=HIGHEST, preferred_element_type=jnp.float32
    )
    block = slot * 4 + row_index
    row = block * B + lax.broadcasted_iota(jnp.int32, (B, B), 0)
    col = col_index * B + lax.broadcasted_iota(jnp.int32, (B, B), 1)
    upper = (row < PIVOTS) & (row < col)
    out_ref[...] = jnp.where(upper, 0.0, total)


def finish(targets, place, front, first, second, base, extra, right):
    slots = front.shape[0] // B
    pieces = base.shape[0] // slots
    return pl.pallas_call(
        finish_kernel,
        grid=(slots,),
        out_shape=jax.ShapeDtypeStruct(front.shape, jnp.float32),
        in_specs=[
            smem_spec(),
            smem_spec(),
            pl.BlockSpec((B, B), lambda s: (s, 0)),
            vmem_spec(),
            vmem_spec(),
            pl.BlockSpec((pieces,) + base.shape[1:], lambda s: (s, 0, 0)),
            vmem_spec(),
            vmem_spec(),
        ],
        out_specs=pl.BlockSpec((B, B), lambda s: (s, 0)),
        scratch_shapes=[pltpu.VMEM((B, PIVOTS), jnp.float32)],
        compiler_params=pltpu.CompilerParams(vmem_limit_bytes=48 << 20),
        name="finish",
    )(targets, place, front, first, second, base, extra, right)


def exchange(value):
    return lax.all_to_all(value, "col", split_axis=0, concat_axis=0, tiled=True)


def on_device(front_entries, child_updates, child_index, child_blocks):
    n_row = lax.axis_size("row")
    n_col = lax.axis_size("col")
    n_cube = lax.axis_size("cube")
    row_index = lax.axis_index("row")
    col_index = lax.axis_index("col")
    cube_index = lax.axis_index("cube")
    sibling = jnp.bitwise_xor(cube_index, 1)
    front = front_entries[0]
    block_lists = jnp.stack([child_index[cube_index, 0], child_index[sibling, 1]])
    counts = jnp.stack([child_blocks[cube_index, 0], child_blocks[sibling, 1]])
    own_block = row_index * n_col + col_index
    targets = lax.dynamic_slice(block_lists, (0, row_index * n_col), (2, n_col))
    place = jnp.concatenate([block_lists[:, own_block], row_index[None], col_index[None]])
    live = jnp.where(own_block < counts, counts, 0)

    turned = front[:B].T
    half = B // 2
    paths = [[], []]
    for part in range(2):
        for source_row in range(PANELS):
            for block in range(n_col):
                source = source_row * n_col + block
                dest = block % n_row * n_col + block // n_row * n_row + source_row * 2 + part
                paths[part].append((source, dest))
    received = [
        lax.ppermute(turned[:, part * half : (part + 1) * half], ("row", "col"), paths[part])
        for part in range(2)
    ]
    own_piece = jnp.where(col_index % 2 == 0, received[0], received[1])
    base = lax.all_gather(own_piece, "col", axis=0, tiled=False)

    swap = [(cube, cube ^ 1) for cube in range(n_cube)]
    arrived_child = lax.ppermute(child_updates[0, 1], "cube", swap)
    spread_first = widen(block_lists[0], live[0:1], child_updates[0, 0])
    spread_second = widen(block_lists[1], live[1:2], arrived_child)

    part = pivot_part(place, spread_first[:PANELS], spread_second[:PANELS], front[:B])
    square = lax.psum(part, ("row", "col"))
    inverse = inverse_factor(square)

    extra_own = jnp.concatenate(
        [
            jnp.concatenate([spread[panel] for panel in range(PANELS)], axis=1)
            for spread in (spread_first, spread_second)
        ],
        axis=0,
    )
    extra = lax.all_gather(extra_own, "col", axis=0, tiled=False)
    first = exchange(spread_first)
    second = exchange(spread_second)
    top = top_rows(targets, front, first, second)
    tops = lax.all_gather(top, "row", axis=0, tiled=False)
    above = tops[:PANELS].reshape(PIVOTS, B)
    solved = jnp.dot(inverse, above, precision=HIGHEST, preferred_element_type=jnp.float32)
    solved = -jnp.dot(inverse.T, solved, precision=HIGHEST, preferred_element_type=jnp.float32)
    own_cols = lax.dynamic_slice_in_dim(inverse, jnp.minimum(col_index, PANELS - 1) * B, B, 0).T
    right = jnp.where(col_index < PANELS, own_cols, solved)
    return finish(targets, place, front, first, second, base, extra, right)[None]


def solution(mesh):
    in_specs = (P("cube", "row", "col"), P("cube", None, ("row", "col"), None), P(), P())
    out_specs = P("cube", "row", "col")
    return jax.shard_map(
        on_device, mesh=mesh, in_specs=in_specs, out_specs=out_specs, check_vma=False
    )
```

time: 1060 us -> 582 us (0.55); the launches traced: 1050 us -> 582 us
  other arithmetic: 334 us -> 3.16 us
  waiting for transfers between devices: 537 us -> 291 us
  Pallas kernels: 0 us -> 198 us
  local copies, waits for them, and re-layouts: 87.2 us -> 35.8 us
  matrix products: 59.1 us -> 17.9 us
  starting transfers between devices: 10.4 us -> 21.5 us
    psum x6 -> x1, waiting for transfers between devices: 447 us -> 176 us  [on_device(): square = lax.psum(part, ('row', 'col'))]
    another operation x35 -> x0, other arithmetic: 239 us -> none  [the longest x29 158 us: on_device(): factor = jnp.linalg.cholesky(pivot_block)]
    pallas_call x0 -> x6, Pallas kernels: none -> 198 us  [the longest x1 160 us: inverse_factor(): pl.pallas_call(inverse_factor_kernel, out_shape=jax.ShapeDtypeStruct((PIV...]
    unnamed x4 -> x0, other arithmetic: 51.1 us -> none
    ppermute x1 -> x3, waiting for transfers between devices: 0.01 us -> 49.9 us  [the longest x2 26.8 us: on_device(): lax.ppermute(turned[:, part * half:(part + 1) * half], ('row', 'col'), pa...]
    another operation x26 -> x0, matrix products: 33.9 us -> none  [the longest x14 29.3 us: solve_panel(): lax.linalg.triangular_solve(factor, rows_in, left_side=False, lower=True,...]
    all_to_all x1 -> x2, waiting for transfers between devices: 90 us -> 64.9 us  [exchange(): return lax.all_to_all(value, 'col', split_axis=0, concat_axis=0, tiled=True)]
    select_n x19 -> x2, other arithmetic: 24 us -> 2.25 us  [the longest x1 1.31 us: on_device(): live = jnp.where(own_block < counts, counts, 0)]
  transfers between devices with their start and end apart: 8 -> 9, of which waited for: 7 -> 6; matrix products, arithmetic and copies ran while one was open for 3% -> 7% of each run, Pallas kernels for 0% -> 29%
where the time goes in v1:
time: 582 us
  waiting for transfers between devices  291 us (50%)
  Pallas kernels  198 us (34%)
  local copies, waits for them, and re-layouts  35.8 us (6%)
  starting transfers between devices  21.5 us (4%)
  matrix products  17.9 us (3%)
  between operations  15.2 us (3%)
    psum x1, waiting for transfers between devices, on_device(): square = lax.psum(part, ('row', 'col'))  176 us
    pallas_call x1, Pallas kernels, inverse_factor(): pl.pallas_call(inverse_factor_kernel, out_shape=jax.ShapeDtypeStruct((PIV...  160 us
    all_to_all x2, waiting for transfers between devices, exchange(): return lax.all_to_all(value, 'col', split_axis=0, concat_axis=0, tiled=True)  64.9 us
    ppermute x2, waiting for transfers between devices, on_device(): lax.ppermute(turned[:, part * half:(part + 1) * half], ('row', 'col'), pa...  26.8 us
    pallas_call x1, Pallas kernels, finish(): pl.pallas_call(finish_kernel, grid=(slots,), out_shape=jax.ShapeDtypeStru...  25.1 us
    ppermute x1, waiting for transfers between devices, on_device(): arrived_child = lax.ppermute(child_updates[0, 1], 'cube', swap)  23.1 us
    unnamed x17, local copies, waits for them, and re-layouts  14 us
    all_to_all x2, starting transfers between devices, exchange(): return lax.all_to_all(value, 'col', split_axis=0, concat_axis=0, tiled=True)  13.2 us
  transfers between devices with their start and end apart: 9, of which 6 were waited for; matrix products, arithmetic and copies ran while one was open for 7% of the time, Pallas kernels for 29%

profile of v1, /device:TPU:97, one launch (start us, length us, event | category | flops | bytes accessed | tf_op | source)
XLA Modules:
  0.0 581.8 jit_solution(1369720369411811768)
XLA Ops:
  7.4 1.4 constant_dynamic-slice_fusion.1
  8.7 1.3 compare_select_fusion
  10.1 0.6 fusion.8
  10.7 0.7 fusion.5
  11.4 1.7 slice_bitcast_fusion
  13.1 4.0 widen.2
  17.0 1.4 copy-done.4
  18.4 8.0 %all-to-all-start = ((f32[16,64,512]{2,1,0:T(8,128)}), f32[16,64,512]{2,1,0:T(8,128)S(1)}, u32[]{:S(2)}, u32[]{:S(2)}) async-start(f32[16,64,512]{2,1,0:T(8,128)} %copy-done.4), calls=%async_computation | async-start | bytes 4194304 | tf_op jit(solution)/shard_map/all_to_all | solution.py:261
  26.4 1.3 collective-permute-start
  27.7 23.1 %collective-permute-done.rows_ref = f32[64,4096]{1,0:T(8,128)S(1)} collective-permute-done((f32[64,4096]{1,0:T(8,128)S(1)}, f32[64,4096]{1,0:T(8,128)S(1)}, u32[]{:S(2)}, u32[]{:S(2)}) %collective-permute-start) | collective-permute-done | bytes 1048608 | tf_op jit(solution)/shard_map/ppermute | solution.py:297
  50.8 4.0 widen.3
  54.8 1.3 copy-done.5
  56.1 19.0 %all-to-all-done.first_ref = f32[16,64,512]{2,1,0:T(8,128)S(1)} async-done(((f32[16,64,512]{2,1,0:T(8,128)}), f32[16,64,512]{2,1,0:T(8,128)S(1)}, u32[]{:S(2)}, u32[]{:S(2)}) %all-to-all-start) | async-done | bytes 2097184 | tf_op jit(solution)/shard_map/all_to_all | solution.py:261
  75.1 5.3 all-to-all-start.1
  80.3 0.0 all-reduce.2.cloned.1.call-start
  80.4 1.0 slice.68.first_ref
  81.3 0.2 fusion.2
  81.5 0.1 pad_add_fusion.1.place_ref
  81.6 1.4 slice_bitcast_fusion.3
  83.0 1.0 slice.69.second_ref
  84.0 0.9 pivot_part.1
  84.8 2.0 copy-done.3
  86.9 0.0 all-gather.11.cloned.1.call-start
  86.9 0.1 constant_dynamic-slice_fusion.3.target_ref
  87.0 46.0 %all-to-all-done.1.second_ref = f32[16,64,512]{2,1,0:T(8,128)} async-done(((f32[16,64,512]{2,1,0:T(8,128)}), f32[16,64,512]{2,1,0:T(8,128)}, u32[]{:S(2)}, u32[]{:S(2)}) %all-to-all-start.1) | async-done | bytes 2097184 | tf_op jit(solution)/shard_map/all_to_all | solution.py:261
  133.0 2.2 copy-done.2
  135.2 3.2 top_rows.1
  138.4 0.0 all-gather.7.cloned.1.call-start
  138.5 1.1 fusion.7
  139.5 4.7 collective-permute-start.1
  144.2 1.9 collective-permute-start.2
  146.2 13.1 %collective-permute-done.1 = f32[512,256]{0,1:T(8,128)S(1)} collective-permute-done((f32[512,256]{0,1:T(8,128)}, f32[512,256]{0,1:T(8,128)S(1)}, u32[]{:S(2)}, u32[]{:S(2)}) %collective-permute-start.1) | collective-permute-done | bytes 524320 | tf_op jit(solution)/shard_map/ppermute | solution.py:290
  159.2 13.8 %collective-permute-done.2 = f32[512,256]{0,1:T(8,128)S(1)} collective-permute-done((f32[512,256]{0,1:T(8,128)}, f32[512,256]{0,1:T(8,128)S(1)}, u32[]{:S(2)}, u32[]{:S(2)}) %collective-permute-start.2) | collective-permute-done | bytes 524320 | tf_op jit(solution)/shard_map/ppermute | solution.py:290
  173.0 0.9 broadcast_select_fusion
  173.9 0.2 all-gather.9.cloned.1.call-start
  174.2 1.0 slice_bitcast_fusion.7
  175.2 1.0 slice_bitcast_fusion.5
  176.1 0.8 maximum_maximum_fusion
  177.0 175.9 %all-reduce.2.cloned.1.call-done.square_ref = f32[1024,1024]{1,0:T(8,128)} async-done(((f32[1024,1024]{1,0:T(8,128)}), f32[1024,1024]{1,0:T(8,128)}) %all-reduce.2.cloned.1.call-update) | async-done | bytes 4194320 | tf_op jit(solution)/shard_map/psum | solution.py:302
  352.9 2.2 copy-done.6
  355.1 160.4 %inverse_factor.1 = f32[1024,1024]{1,0:T(8,128)S(1)} custom-call(f32[1024,1024]{1,0:T(8,128)S(1)} %copy-done.6), custom_call_target="tpu_custom_call" | custom-call | tf_op jit(solution)/shard_map/inverse_factor/pallas_call | solution.py:161
  515.5 2.0 copy-done
  517.6 1.6 constant_dynamic-slice_fusion
  519.2 2.9 copy.9
  522.1 9.6 %fusion = f32[1024,512]{1,0:T(8,128)S(1)} fusion(f32[1024,1024]{1,0:T(8,128)} %copy-done, f32[2048,512]{1,0:T(8,128)} %all-gather.11.cloned.1.call-done), kind=kOutput, calls=%fused_computation | convolution fusion | flops 6442450944 | bytes 8388608 | tf_op jit(solution)/shard_map/dot_general | solution.py:318
  531.8 8.2 %bitcast_select_fusion.right_ref = f32[1024,512]{1,0:T(8,128)} fusion(f32[512,1024]{0,1:T(8,128)S(1)} %copy-done.7, f32[1024,1024]{1,0:T(8,128)S(1)} %copy-done.1, f32[1024,512]{1,0:T(8,128)S(1)} %fusion, pred[]{:T(512)S(6)} %lt.39), kind=kOutput, calls=%fused_computation.2 | convolution fusion | flops 6443499520 | bytes 10485761 | tf_op jit(solution)/shard_map/dot_general | solution.py:319
  540.0 9.1 %copy.7 = f32[8192,256]{1,0:T(8,128)} copy(f32[8192,256]{0,1:T(8,128)} %all-gather.7.cloned.1.call-done) | data formatting | bytes 16777216 | tf_op jit(solution)/shard_map/all_gather | solution.py:294
  549.1 25.1 %finish.1 = f32[2048,512]{1,0:T(8,128)} custom-call(s32[2,16]{1,0:T(2,128)S(1)} %constant_dynamic-slice_fusion.3.target_ref, s32[4]{0:T(128)S(1)} %pad_add_fusion.1.place_ref, f32[2048,512]{1,0:T(8,128)} %bitcast.38, f32[16,64,512]{2,1,0:T(8,128)S(1)} %all-to-all-done.first_ref, f32[16,64,512]{2,1,0:T(8,128)} %all-to-all-done.1.second_ref, ...), custom_call_target="tpu_custom_call" | custom-call | tf_op jit(solution)/shard_map/finish/pallas_call | solution.py:239
  (18 shorter events, 0.1 us)
Async XLA Ops:
  17.0 1.4 copy-start.4
  18.4 56.7 %all-to-all-start = ((f32[16,64,512]{2,1,0:T(8,128)}), f32[16,64,512]{2,1,0:T(8,128)S(1)}, u32[]{:S(2)}, u32[]{:S(2)}) async-start(f32[16,64,512]{2,1,0:T(8,128)} %copy-done.4), calls=%async_computation | async-start | bytes 4194304 | tf_op jit(solution)/shard_map/all_to_all | solution.py:261
  26.4 24.4 %collective-permute-start = (f32[64,4096]{1,0:T(8,128)S(1)}, f32[64,4096]{1,0:T(8,128)S(1)}, u32[]{:S(2)}, u32[]{:S(2)}) collective-permute-start(f32[64,4096]{1,0:T(8,128)S(1)} %get-tuple-element.11), channel_id=1, source_target_pairs={{0,64},{64,0},{128,192},{192,128},{1,65},{65,1},{129,193},{193,129... | collective-permute-start | bytes 3145736 | tf_op jit(solution)/shard_map/ppermute | solution.py:297
  54.8 1.3 copy-start.5
  75.1 57.9 %all-to-all-start.1 = ((f32[16,64,512]{2,1,0:T(8,128)}), f32[16,64,512]{2,1,0:T(8,128)}, u32[]{:S(2)}, u32[]{:S(2)}) async-start(f32[16,64,512]{2,1,0:T(8,128)} %copy-done.5), calls=%async_computation.1 | async-start | bytes 4194304 | tf_op jit(solution)/shard_map/all_to_all | solution.py:261
  80.3 272.6 %all-reduce.2.cloned.1.call-start = ((), (), s32[]{:S(2)}) async-start(), calls=%async_computation.2 | async-start | bytes 8388608 | tf_op jit(solution)/shard_map/psum | solution.py:302
  84.8 2.0 copy-start.3
  86.9 435.3 %all-gather.11.cloned.1.call-start = ((), (), s32[]{:S(2)}) async-start(), calls=%async_computation.5 | async-start | bytes 5242880 | tf_op jit(solution)/shard_map/all_gather | solution.py:316
  133.0 2.2 copy-start.2
  138.4 401.6 %all-gather.7.cloned.1.call-start = ((), (), s32[]{:S(2)}) async-start(), calls=%async_computation.3 | async-start | bytes 8912896 | tf_op jit(solution)/shard_map/all_gather | solution.py:294
  139.5 19.7 %collective-permute-start.1 = (f32[512,256]{0,1:T(8,128)}, f32[512,256]{0,1:T(8,128)S(1)}, u32[]{:S(2)}, u32[]{:S(2)}) collective-permute-start(f32[512,256]{0,1:T(8,128)} %get-tuple-element.14), channel_id=1, source_target_pairs={{0,0},{1,16},{2,32},{3,48},{4,4},{5,20},{6,36},{7,52},{8,8},{9,24}... | collective-permute-start | bytes 1572872 | tf_op jit(solution)/shard_map/ppermute | solution.py:290
  144.2 28.8 %collective-permute-start.2 = (f32[512,256]{0,1:T(8,128)}, f32[512,256]{0,1:T(8,128)S(1)}, u32[]{:S(2)}, u32[]{:S(2)}) collective-permute-start(f32[512,256]{0,1:T(8,128)} %get-tuple-element.13), channel_id=1, source_target_pairs={{0,1},{1,17},{2,33},{3,49},{4,5},{5,21},{6,37},{7,53},{8,9},{9,25}... | collective-permute-start | bytes 1572872 | tf_op jit(solution)/shard_map/ppermute | solution.py:290
  173.9 375.2 %all-gather.9.cloned.1.call-start = ((), (), s32[]{:S(2)}) async-start(), calls=%async_computation.4 | async-start | bytes 8912896 | tf_op jit(solution)/shard_map/all_gather | solution.py:312
  352.9 2.2 copy-start.6
  515.5 2.0 copy-start
  522.1 9.7 %copy-start.1 = (f32[1024,1024]{1,0:T(8,128)S(1)}, f32[1024,1024]{1,0:T(8,128)}, u32[]{:S(2)}) copy-start(f32[1024,1024]{1,0:T(8,128)} %copy-done) | copy-start | bytes 12582916
  522.1 9.7 %copy-start.7 = (f32[512,1024]{0,1:T(8,128)S(1)}, f32[512,1024]{0,1:T(8,128)}, u32[]{:S(2)}) copy-start(f32[512,1024]{0,1:T(8,128)} %copy.9) | copy-start | bytes 6291460
Sparse Core Ops, SparseCore 0:
  87.0 265.8 all-reduce.1
Sparse Core Ops, SparseCore 1:
  138.5 66.0 all-gather.10
  206.2 54.1 all-gather.6
  262.1 56.9 all-gather.8

commit v2 on v0

v2 whole, which is shorter than its diff:
```python
import jax
import jax.numpy as jnp
from jax import lax
from jax.experimental import pallas as pl
from jax.experimental.pallas import tpu as pltpu
from jax.sharding import PartitionSpec as P

F = 8192
B = 512
SBLK = 64
CR = 4096
PANELS = 2
PIVOTS = PANELS * B
PER_PANEL = B // SBLK
TILE = 128
GROUP = 8
HIGHEST = lax.Precision.HIGHEST
VMEM = pltpu.VMEM
SMEM = pltpu.SMEM


def vmem_spec():
    return pl.BlockSpec(memory_space=VMEM)


def smem_spec():
    return pl.BlockSpec(memory_space=SMEM)


def cost(seconds, moved):
    return pl.CostEstimate(flops=int(seconds * 1e15), bytes_accessed=moved, transcendentals=0)


def widen_kernel(list_ref, live_ref, first_ref, second_ref, out_ref):
    out_ref[...] = jnp.zeros_like(out_ref)
    lane = lax.broadcasted_iota(jnp.int32, (SBLK, TILE), 1)
    for child, rows_ref in enumerate((first_ref, second_ref)):
        out_rows = slice(child * SBLK, (child + 1) * SBLK)

        def place(pair, carry):
            both = rows_ref[:, pl.ds(pl.multiple_of(pair * TILE, TILE), TILE)]
            other = pltpu.roll(both, SBLK, 1)
            for half in range(2):
                block = pair * 2 + half
                target = list_ref[child, block]
                parity = target % 2
                offset = pl.multiple_of(target % PER_PANEL // 2 * TILE, TILE)
                owner = target // PER_PANEL
                moved = jnp.where(parity == half, both, other)
                keep = (lane // SBLK == parity) & (block < live_ref[child])
                spot = (owner, out_rows, pl.ds(offset, TILE))
                out_ref[spot] = jnp.where(keep, moved, out_ref[spot])
            return carry

        lax.fori_loop(0, CR // TILE, place, 0)


def widen(lists, live, first, second):
    return pl.pallas_call(
        widen_kernel,
        out_shape=jax.ShapeDtypeStruct((F // B, 2 * SBLK, B), jnp.float32),
        in_specs=[smem_spec(), smem_spec(), vmem_spec(), vmem_spec()],
        out_specs=vmem_spec(),
        compiler_params=pltpu.CompilerParams(vmem_limit_bytes=16 << 20),
        cost_estimate=cost(8e-6, 6 << 20),
        name="widen",
    )(lists, live, first, second)


def pick_kernel(list_ref, live_ref, rows_ref, first_ref, second_ref):
    lane = lax.broadcasted_iota(jnp.int32, (SBLK, TILE), 1)
    for child, out_ref in enumerate((first_ref, second_ref)):
        out_ref[...] = jnp.zeros_like(out_ref)
        for pair in range(rows_ref.shape[2] // TILE):
            both = rows_ref[child, :, pair * TILE : (pair + 1) * TILE]
            other = pltpu.roll(both, SBLK, 1)
            for half in range(2):
                block = pair * 2 + half
                target = list_ref[child, block]

                @pl.when((target < PANELS * PER_PANEL) & (block < live_ref[child]))
                def _():
                    parity = target % 2
                    moved = jnp.where(parity == half, both, other)
                    spot = pl.ds(pl.multiple_of(target // 2 * TILE, TILE), TILE)
                    out_ref[:, spot] = jnp.where(lane // SBLK == parity, moved, out_ref[:, spot])


def pick(lists, live, rows):
    width = PANELS * CR // 4
    return pl.pallas_call(
        pick_kernel,
        grid=(1,),
        out_shape=[jax.ShapeDtypeStruct((SBLK, PIVOTS), jnp.float32)] * 2,
        in_specs=[smem_spec(), smem_spec(), pl.BlockSpec((2, SBLK, width), lambda i: (0, 0, 0))],
        out_specs=[pl.BlockSpec((SBLK, PIVOTS), lambda i: (0, 0))] * 2,
        compiler_params=pltpu.CompilerParams(vmem_limit_bytes=16 << 20),
        cost_estimate=cost(3e-6, 2 << 20),
        name="pick",
    )(lists, live, rows)


def pivot_block(owner):
    return owner % PANELS * PER_PANEL + owner // PANELS


def turn_kernel(first_ref, second_ref, out_ref):
    half = SBLK // 2
    for child, source in enumerate((first_ref, second_ref)):
        turned = source[...].T
        for owner in range(out_ref.shape[0]):
            at = pivot_block(owner) * SBLK
            out_ref[owner, child] = jnp.concatenate(
                [turned[at : at + half], turned[at + half : at + SBLK]], axis=1
            )


def turn(first, second):
    owners = PIVOTS // SBLK
    return pl.pallas_call(
        turn_kernel,
        out_shape=jax.ShapeDtypeStruct((owners, 2, SBLK // 2, 2 * SBLK), jnp.float32),
        in_specs=[vmem_spec()] * 2,
        out_specs=vmem_spec(),
        cost_estimate=cost(2e-6, 1 << 20),
        name="turn",
    )(first, second)


def chunk_kernel(target_ref, place_ref, *refs):
    base_refs, first_ref, second_ref, out_ref = refs[:-3], refs[-3], refs[-2], refs[-1]
    steps = len(base_refs)
    half = SBLK // 2
    own_piece = place_ref[1] // PANELS
    for slot in range(out_ref.shape[1] // B):
        for step in range(steps):

            @pl.when((step + 2 * slot) % steps == own_piece)
            def _():
                out_ref[:, slot * B : (slot + 1) * B] = base_refs[step][...]

    lane = lax.broadcasted_iota(jnp.int32, (half, TILE), 1)
    for child, source in enumerate((first_ref, second_ref)):
        for t in range(source.shape[0]):
            both = source[t]
            other = pltpu.roll(both, SBLK, 1)
            target = target_ref[child, t]
            parity = target % 2
            offset = target // (PER_PANEL * 4) * B + target % PER_PANEL // 2 * TILE
            spot = pl.ds(pl.multiple_of(offset, TILE), TILE)
            keep = lane // SBLK == parity
            for part in range(2):
                rows = slice(part * half, (part + 1) * half)
                moved = jnp.where(parity == part, both, other)
                out_ref[rows, spot] = out_ref[rows, spot] + jnp.where(keep, moved, 0.0)


def chunk(targets, place, base, first, second, width):
    return pl.pallas_call(
        chunk_kernel,
        out_shape=jax.ShapeDtypeStruct((SBLK, width), jnp.float32),
        in_specs=[smem_spec(), smem_spec()] + [vmem_spec()] * (len(base) + 2),
        out_specs=vmem_spec(),
        cost_estimate=cost(3e-6, 2 << 20),
        name="chunk",
    )(targets, place, *base, first, second)


def spread_over(value):
    return jnp.broadcast_to(value, (GROUP, TILE))


def inverse_factor_tile(tile):
    count = TILE // GROUP
    groups = [tile[GROUP * g : GROUP * g + GROUP, :] for g in range(count)]
    lane = lax.broadcasted_iota(jnp.int32, (GROUP, TILE), 1)
    sub = lax.broadcasted_iota(jnp.int32, (GROUP, TILE), 0)
    done = []
    for g in range(count):
        first = GROUP * g
        here = lane // GROUP == g
        own = groups[g]
        cols = [
            [spread_over(groups[i][:, first + q : first + q + 1]) for q in range(GROUP)]
            for i in range(g, count)
        ]
        square = [
            [spread_over(cols[0][q][i : i + 1, :]) if i >= q else None for q in range(GROUP)]
            for i in range(GROUP)
        ]
        rows = [
            jnp.where(here, jnp.where(lane == first + q, 1.0, 0.0), spread_over(own[q : q + 1, :]))
            for q in range(GROUP)
        ]
        ratio = [[None] * GROUP for _ in range(GROUP)]
        recip = [None] * GROUP
        result = None
        for q in range(GROUP):
            pivot = square[q][q]
            recip[q] = 1.0 / pivot
            for i in range(q + 1, GROUP):
                ratio[i][q] = square[i][q] * recip[q]
            for i in range(q + 1, GROUP):
                for j in range(q + 1, i + 1):
                    square[i][j] = square[i][j] - ratio[i][q] * square[j][q]
            for i in range(q + 1, GROUP):
                rows[i] = rows[i] - ratio[i][q] * rows[q]
            root = lax.rsqrt(pivot)
            root = root * (1.5 - 0.5 * pivot * root * root)
            scaled = rows[q] * root
            result = scaled if result is None else jnp.where(sub == q, scaled, result)
        done.append(jnp.where(lane <= sub + first, result, 0.0))
        if g + 1 < count:
            back = [None] * GROUP
            for q in reversed(range(GROUP)):
                back[q] = rows[q] * recip[q]
                for k in range(q + 1, GROUP):
                    back[q] = back[q] - ratio[k][q] * back[k]
            for i in range(g + 1, count):
                value = jnp.where(here, 0.0, groups[i])
                for q in range(GROUP):
                    value = value - cols[i - g][q] * back[q]
                groups[i] = value
    return jnp.concatenate(done, axis=0)


def inverse_factor_kernel(square_ref, inv_ref, row_ref):
    for owner in range(PIVOTS // SBLK):
        at = pivot_block(owner) * SBLK
        inv_ref[at : at + SBLK, :] = square_ref[owner * SBLK : (owner + 1) * SBLK, :]
    lane = lax.broadcasted_iota(jnp.int32, (TILE, TILE), 1)
    sub = lax.broadcasted_iota(jnp.int32, (TILE, TILE), 0)
    identity = jnp.where(lane == sub, 1.0, 0.0)
    steps = PIVOTS // TILE

    def step(k, carry):
        at = pl.ds(pl.multiple_of(k * TILE, TILE), TILE)
        inv_tile = inverse_factor_tile(inv_ref[at, at])
        inv_ref[at, at] = identity
        row_ref[...] = jnp.dot(
            inv_tile, inv_ref[at, :], precision=HIGHEST, preferred_element_type=jnp.float32
        )
        inv_ref[at, :] = row_ref[...]

        def below(i, carry):
            rows = pl.ds(pl.multiple_of(i * TILE, TILE), TILE)
            left = row_ref[:, rows]
            inv_ref[rows, at] = jnp.zeros((TILE, TILE), jnp.float32)
            inv_ref[rows, :] = inv_ref[rows, :] - lax.dot_general(
                left,
                row_ref[...],
                (((0,), (0,)), ((), ())),
                precision=HIGHEST,
                preferred_element_type=jnp.float32,
            )
            return carry

        return lax.fori_loop(k + 1, steps, below, carry)

    lax.fori_loop(0, steps, step, 0)
    for k in range(steps - 1):
        rows = slice(k * TILE, k * TILE + TILE)
        inv_ref[rows, (k + 1) * TILE :] = jnp.zeros((TILE, PIVOTS - (k + 1) * TILE), jnp.float32)


def inverse_factor(gathered):
    return pl.pallas_call(
        inverse_factor_kernel,
        grid=(1,),
        out_shape=jax.ShapeDtypeStruct((PIVOTS, PIVOTS), jnp.float32),
        in_specs=[pl.BlockSpec((PIVOTS, PIVOTS), lambda i: (0, 0))],
        out_specs=pl.BlockSpec((PIVOTS, PIVOTS), lambda i: (0, 0)),
        scratch_shapes=[pltpu.VMEM((TILE, PIVOTS), jnp.float32)],
        compiler_params=pltpu.CompilerParams(vmem_limit_bytes=56 << 20),
        cost_estimate=cost(70e-6, 8 << 20),
        name="inverse_factor",
    )(gathered)


def split(value):
    high = value.astype(jnp.bfloat16)
    return high, (value - high.astype(jnp.float32)).astype(jnp.bfloat16)


def keep_right(high_ref, low_ref, value, start, cols):
    high, low = split(value)
    for owner in range(PIVOTS // SBLK):
        at = pivot_block(owner) * SBLK - start
        if 0 <= at < value.shape[0]:
            rows = slice(owner * SBLK, (owner + 1) * SBLK)
            high_ref[rows, cols] = high[at : at + SBLK]
            low_ref[rows, cols] = low[at : at + SBLK]


def from_left(left, right):
    return lax.dot_general(
        left, right, (((0,), (0,)), ((), ())), preferred_element_type=jnp.float32
    )


def finish_kernel(
    place_ref, front_ref, left_ref, inv_ref, *refs
):
    above_refs, (out_ref, above_ref, solved_ref, high_ref, low_ref, sem) = refs[:-6], refs[-6:]
    slot = pl.program_id(0)
    row_index, col_index = place_ref[0], place_ref[1]
    trailing = col_index >= PANELS
    step = 256

    @pl.when((slot == 0) & trailing)
    def _():
        n_row = len(above_refs)
        away = (row_index + n_row - col_index % n_row) % n_row
        for index, source in enumerate(above_refs):

            @pl.when(away == index)
            def _():
                copies = []
                for owner in range(PIVOTS // SBLK):
                    at = pivot_block(owner) * SBLK
                    copies.append(
                        pltpu.make_async_copy(
                            source.at[owner * SBLK : (owner + 1) * SBLK, :],
                            above_ref.at[at : at + SBLK, :],
                            sem.at[owner],
                        )
                    )
                for copy in copies:
                    copy.start()
                for copy in copies:
                    copy.wait()

        for i in range(PIVOTS // step):
            rows = slice(i * step, (i + 1) * step)
            solved_ref[rows, :] = jnp.dot(
                inv_ref[rows, : (i + 1) * step],
                above_ref[: (i + 1) * step, :],
                precision=HIGHEST,
                preferred_element_type=jnp.float32,
            )
        for j in range(PIVOTS // step):
            rows = slice(j * step, (j + 1) * step)
            value = -lax.dot_general(
                inv_ref[j * step :, rows],
                solved_ref[j * step :, :],
                (((0,), (0,)), ((), ())),
                precision=HIGHEST,
                preferred_element_type=jnp.float32,
            )
            keep_right(high_ref, low_ref, value, j * step, slice(None))

    @pl.when((slot == 0) & jnp.logical_not(trailing))
    def _():
        for part in range(B // TILE):
            cols = slice(part * TILE, (part + 1) * TILE)
            own = pl.ds(pl.multiple_of(col_index * B + part * TILE, TILE), TILE)
            keep_right(high_ref, low_ref, inv_ref[own, :].T, 0, cols)

    left_high, left_low = split(left_ref[...])
    total = from_left(left_low, high_ref[...]) + from_left(left_high, low_ref[...])
    total = total + from_left(left_high, high_ref[...])
    out_ref[...] = total + jnp.where(trailing, front_ref[...], 0.0)

    @pl.when(slot == 0)
    def _():
        row = row_index * B + lax.broadcasted_iota(jnp.int32, (B, B), 0)
        col = col_index * B + lax.broadcasted_iota(jnp.int32, (B, B), 1)
        out_ref[...] = jnp.where((row < PIVOTS) & (row < col), 0.0, out_ref[...])


def finish(place, front, gathered, inverse, above):
    slots = front.shape[0] // B
    return pl.pallas_call(
        finish_kernel,
        grid=(slots,),
        out_shape=jax.ShapeDtypeStruct(front.shape, jnp.float32),
        in_specs=[
            smem_spec(),
            pl.BlockSpec((B, B), lambda s: (s, 0)),
            pl.BlockSpec((PIVOTS, B), lambda s: (0, s + PANELS)),
            vmem_spec(),
        ]
        + [pl.BlockSpec(memory_space=pl.ANY)] * len(above),
        out_specs=pl.BlockSpec((B, B), lambda s: (s, 0)),
        scratch_shapes=[
            pltpu.VMEM((PIVOTS, B), jnp.float32),
            pltpu.VMEM((PIVOTS, B), jnp.float32),
            pltpu.VMEM((PIVOTS, B), jnp.bfloat16),
            pltpu.VMEM((PIVOTS, B), jnp.bfloat16),
            pltpu.SemaphoreType.DMA((PIVOTS // SBLK,)),
        ],
        compiler_params=pltpu.CompilerParams(vmem_limit_bytes=40 << 20),
        cost_estimate=cost(22e-6, 26 << 20),
        name="finish",
    )(place, front, gathered, inverse, *above)


def land_kernel(target_ref, place_ref, part_ref, source_ref, out_ref):
    slot = pl.program_id(0)
    row_index, col_index = place_ref[0], place_ref[1]
    out_ref[...] = part_ref[...]

    @pl.when((col_index >= PANELS) & (slot * 4 + row_index >= PANELS))
    def _():
        for child in range(source_ref.shape[1] // SBLK):
            for t in range(source_ref.shape[0]):
                target = target_ref[child, t]

                @pl.when(target // (PER_PANEL * 4) == slot)
                def _():
                    rows = pl.ds(pl.multiple_of(target % PER_PANEL * SBLK, SBLK), SBLK)
                    at = slice(child * SBLK, (child + 1) * SBLK)
                    out_ref[rows, :] = out_ref[rows, :] + source_ref[t, at]


def land(targets, place, part, source):
    slots = part.shape[0] // B
    return pl.pallas_call(
        land_kernel,
        grid=(slots,),
        out_shape=jax.ShapeDtypeStruct(part.shape, jnp.float32),
        in_specs=[
            smem_spec(),
            smem_spec(),
            pl.BlockSpec((B, B), lambda s: (s, 0)),
            vmem_spec(),
        ],
        out_specs=pl.BlockSpec((B, B), lambda s: (s, 0)),
        input_output_aliases={2: 0},
        compiler_params=pltpu.CompilerParams(vmem_limit_bytes=16 << 20),
        cost_estimate=cost(5e-6, 12 << 20),
        name="land",
    )(targets, place, part, source)


def exchange(value):
    return lax.all_to_all(value, "col", split_axis=0, concat_axis=0, tiled=True)


def front_pieces(top, n_row, n_col, col_index):
    steps = B // SBLK
    received = []
    for step in range(steps):
        paths = []
        for panel in range(PANELS):
            for block in range(n_col):
                piece = (step + 2 * (block // n_row)) % steps
                paths.append((panel * n_col + block, block % n_row * n_col + piece * PANELS + panel))
        moved = []
        for slot in range(n_col // n_row):
            piece = (step + 2 * slot) % steps
            moved.append(top[piece * SBLK : (piece + 1) * SBLK])
        own_slot = col_index // n_row
        value = moved[0]
        for slot in range(1, n_col // n_row):
            value = jnp.where(own_slot == slot, moved[slot], value)
        received.append(lax.ppermute(value, ("row", "col"), paths))
    return received


def share_above(own, n_row, n_col):
    pieces = [own]
    for away in range(1, n_row):
        paths = []
        for col in range(n_col):
            root = col % n_row
            paths.append((root * n_col + col, (root + away) % n_row * n_col + col))
        pieces.append(lax.ppermute(own, ("row", "col"), paths))
    return pieces


def share_heads(own, n_row, row_index):
    moved = [own]
    for away in range(1, n_row):
        paths = [(row, (row + away) % n_row) for row in range(PANELS)]
        if away == n_row - 1:
            paths = [(0, n_row - 1), (1, 0)]
        moved.append(lax.ppermute(own, "row", paths))
    heads = []
    for panel in range(PANELS):
        value = moved[0]
        for away in range(1, n_row):
            value = jnp.where((row_index - panel) % n_row == away, moved[away], value)
        heads.append(value)
    return heads


def on_device(front_entries, child_updates, child_index, child_blocks):
    n_row = lax.axis_size("row")
    n_col = lax.axis_size("col")
    n_cube = lax.axis_size("cube")
    row_index = lax.axis_index("row")
    col_index = lax.axis_index("col")
    cube_index = lax.axis_index("cube")
    sibling = jnp.bitwise_xor(cube_index, 1)
    front = front_entries[0]
    own_block = row_index * n_col + col_index
    own_lists = child_index[cube_index]
    own_counts = child_blocks[cube_index]
    own_live = jnp.where(own_block < own_counts, own_counts, 0)
    block_lists = jnp.stack([own_lists[0], child_index[sibling, 1]])
    counts = jnp.stack([own_counts[0], child_blocks[sibling, 1]])
    live = jnp.where(own_block < counts, counts, 0)
    targets = lax.dynamic_slice(block_lists, (0, row_index * n_col), (2, n_col))
    place = jnp.stack([row_index, col_index])
    swap = [(cube, cube ^ 1) for cube in range(n_cube)]

    base = front_pieces(front[:B], n_row, n_col, col_index)
    picked_first, picked_second = pick(own_lists, own_live, child_updates[0])
    turned = exchange(turn(picked_first, picked_second))
    turned_second = lax.ppermute(turned[:, 1], "cube", swap)
    own_chunk = chunk(targets, place, base, turned[:, 0], turned_second, front.shape[0])
    heads = share_heads(own_chunk[:, :B], n_row, row_index)
    own_chunk = jnp.concatenate(heads + [own_chunk], axis=1)
    gathered = lax.all_gather(own_chunk, "col", axis=0, tiled=True)

    arrived_child = lax.ppermute(child_updates[0, 1], "cube", swap)
    spread = widen(block_lists, live, child_updates[0, 0], arrived_child)
    gathered, spread = lax.optimization_barrier((gathered, spread))
    arrived = exchange(spread)

    own_above = lax.dynamic_slice(
        gathered, (0, PIVOTS + col_index // n_row * B), (PIVOTS, B)
    )
    above = share_above(own_above, n_row, n_col)
    inverse = inverse_factor(gathered)
    part = finish(place, front, gathered, inverse, above)
    return land(targets, place, part, arrived)[None]


def solution(mesh):
    in_specs = (P("cube", "row", "col"), P("cube", None, ("row", "col"), None), P(), P())
    out_specs = P("cube", "row", "col")
    return jax.shard_map(
        on_device, mesh=mesh, in_specs=in_specs, out_specs=out_specs, check_vma=False
    )
```

time: 1060 us -> 297 us (0.28)
  waiting for transfers between devices: 537 us -> 80.6 us
  other arithmetic: 334 us -> 7.75 us
  Pallas kernels: 0 us -> 120 us
  local copies, waits for them, and re-layouts: 87.2 us -> 15.2 us
  matrix products: 59.1 us -> 0 us
  starting transfers between devices: 10.4 us -> 56.8 us
    psum x6 -> x0, waiting for transfers between devices: 447 us -> none  [the longest x4 348 us: spread_2(): return lax.psum(block, axis)]
    another operation x36 -> x2, other arithmetic: 239 us -> 0.6 us  [the longest x1 0.6 us: on_device(): place = jnp.stack([row_index, col_index])]
    pallas_call x0 -> x7, Pallas kernels: none -> 120 us  [the longest x1 76.9 us: inverse_factor(): pl.pallas_call(inverse_factor_kernel, grid=(1,), out_shape=jax.ShapeDtype...]
    all_to_all x1 -> x2, waiting for transfers between devices: 90 us -> 0.01 us  [exchange(): return lax.all_to_all(value, 'col', split_axis=0, concat_axis=0, tiled=True)]
    unnamed x4 -> x0, other arithmetic: 51.1 us -> none
    all_gather x0 -> x1, waiting for transfers between devices: none -> 45.3 us  [on_device(): gathered = lax.all_gather(own_chunk, 'col', axis=0, tiled=True)]
    ppermute x1 -> x16, starting transfers between devices: 1.3 us -> 37.7 us  [the longest x8 23.2 us: front_pieces(): received.append(lax.ppermute(value, ('row', 'col'), paths))]
    ppermute x1 -> x16, waiting for transfers between devices: 0.01 us -> 35.3 us  [the longest x1 19.4 us: on_device(): arrived_child = lax.ppermute(child_updates[0, 1], 'cube', swap)]
  transfers between devices with their start and end apart: 8 -> 19, of which waited for: 7 -> 9; matrix products, arithmetic and copies ran while one was open for 3% -> 3% of each run, Pallas kernels for 0% -> 36%
where the time goes in v2:
time: 297 us; the launch traced here: 294 us
  Pallas kernels  120 us (40%)
  waiting for transfers between devices  80.6 us (27%)
  starting transfers between devices  56.8 us (19%)
  local copies, waits for them, and re-layouts  15.2 us (5%)
  between operations  13.8 us (5%)
  other arithmetic  7.75 us (3%)
    pallas_call x1, Pallas kernels, inverse_factor(): pl.pallas_call(inverse_factor_kernel, grid=(1,), out_shape=jax.ShapeDtype...  76.9 us
    all_gather x1, waiting for transfers between devices, on_device(): gathered = lax.all_gather(own_chunk, 'col', axis=0, tiled=True)  45.3 us
    ppermute x8, starting transfers between devices, front_pieces(): received.append(lax.ppermute(value, ('row', 'col'), paths))  23.2 us
    pallas_call x1, Pallas kernels, finish(): pl.pallas_call(finish_kernel, grid=(slots,), out_shape=jax.ShapeDtypeStru...  22.1 us
    ppermute x1, waiting for transfers between devices, on_device(): arrived_child = lax.ppermute(child_updates[0, 1], 'cube', swap)  19.4 us
    all_to_all x2, starting transfers between devices, exchange(): return lax.all_to_all(value, 'col', split_axis=0, concat_axis=0, tiled=True)  19.1 us
    ppermute x8, waiting for transfers between devices, front_pieces(): received.append(lax.ppermute(value, ('row', 'col'), paths))  12.1 us
    pallas_call x1, Pallas kernels, land(): pl.pallas_call(land_kernel, grid=(slots,), out_shape=jax.ShapeDtypeStruct...  6.79 us
  transfers between devices with their start and end apart: 19, of which 9 were waited for; matrix products, arithmetic and copies ran while one was open for 3% of the time, Pallas kernels for 36%

profile of v2, /device:TPU:97, one launch (start us, length us, event | category | flops | bytes accessed | tf_op | source)
XLA Modules:
  0.0 294.2 jit_solution(11375285926957649893)
XLA Ops:
  7.2 0.9 fusion.13
  8.1 1.6 copy-done.1
  9.7 3.1 %pick.1 = (f32[64,1024]{1,0:T(8,128)S(1)}, f32[64,1024]{1,0:T(8,128)S(1)}) custom-call(s32[2,64]{1,0:T(2,128)S(1)} %fusion.14.list_ref, s32[2]{0:T(128)S(1)} %compare_select_fusion.1.live_ref, f32[2,64,4096]{2,1,0:T(8,128)S(1)} %bitcast.97), custom_call_target="tpu_custom_call" | custom-call | flops 3000000000 | bytes 2097152 | tf_op jit(solution)/shard_map/pick/pallas_call | solution.py:91
  12.7 0.7 copy-done.6
  13.5 0.7 copy-done.7
  14.2 2.3 turn.1
  16.5 8.0 %all-to-all-start = ((f32[16,2,32,128]{3,2,1,0:T(8,128)}), f32[16,2,32,128]{3,2,1,0:T(8,128)S(1)}, u32[]{:S(2)}, u32[]{:S(2)}) async-start(f32[16,2,32,128]{3,2,1,0:T(8,128)} %turn.1), calls=%async_computation | async-start | bytes 1048576 | tf_op jit(solution)/shard_map/all_to_all | solution.py:437
  24.5 1.4 fusion.10
  25.9 4.1 %collective-permute-start.6 = (f32[64,512]{1,0:T(8,128)S(1)}, f32[64,512]{1,0:T(8,128)S(1)}, u32[]{:S(2)}, u32[]{:S(2)}) collective-permute-start(f32[64,512]{1,0:T(8,128)S(1)} %get-tuple-element.19), channel_id=1, source_target_pairs={{0,12},{1,28},{2,44},{3,60},{4,0},{5,16},{6,32},{7,48},{8,4},{9,20... | collective-permute-start | bytes 393224 | tf_op jit(solution)/shard_map/ppermute | solution.py:457
  30.1 3.9 %collective-permute-start.4 = (f32[64,512]{1,0:T(8,128)S(1)}, f32[64,512]{1,0:T(8,128)S(1)}, u32[]{:S(2)}, u32[]{:S(2)}) collective-permute-start(f32[64,512]{1,0:T(8,128)S(1)} %get-tuple-element.20), channel_id=1, source_target_pairs={{0,8},{1,24},{2,40},{3,56},{4,12},{5,28},{6,44},{7,60},{8,0},{9,16... | collective-permute-start | bytes 393224 | tf_op jit(solution)/shard_map/ppermute | solution.py:457
  33.9 1.3 collective-permute-start.2
  35.2 1.9 collective-permute-start.1
  38.5 1.4 fusion.4
  39.9 0.8 slice_bitcast_fusion.2
  40.7 1.3 collective-permute-start.8
  42.0 3.7 %collective-permute-start.7 = (f32[64,512]{1,0:T(8,128)S(1)}, f32[64,512]{1,0:T(8,128)S(1)}, u32[]{:S(2)}, u32[]{:S(2)}) collective-permute-start(f32[64,512]{1,0:T(8,128)S(1)} %get-tuple-element.15), channel_id=1, source_target_pairs={{0,14},{1,30},{2,46},{3,62},{4,2},{5,18},{6,34},{7,50},{8,6},{9,22... | collective-permute-start | bytes 393224 | tf_op jit(solution)/shard_map/ppermute | solution.py:457
  45.7 4.2 %collective-permute-done.4.refs_4_ = f32[64,512]{1,0:T(8,128)S(1)} collective-permute-done((f32[64,512]{1,0:T(8,128)S(1)}, f32[64,512]{1,0:T(8,128)S(1)}, u32[]{:S(2)}, u32[]{:S(2)}) %collective-permute-start.4) | collective-permute-done | bytes 131104 | tf_op jit(solution)/shard_map/ppermute | solution.py:457
  50.0 1.9 collective-permute-start.5
  51.9 1.3 collective-permute-done.2.refs_2_
  53.2 1.9 collective-permute-start.3
  55.1 4.5 %collective-permute-start = (f32[64,512]{1,0:T(8,128)S(1)}, f32[64,512]{1,0:T(8,128)S(1)}, u32[]{:S(2)}, u32[]{:S(2)}) collective-permute-start(f32[64,512]{1,0:T(8,128)S(1)} %get-tuple-element.18), channel_id=1, source_target_pairs={{0,0},{1,16},{2,32},{3,48},{4,4},{5,20},{6,36},{7,52},{8,8},{9,24}... | collective-permute-start | bytes 393224 | tf_op jit(solution)/shard_map/ppermute | solution.py:457
  60.8 1.3 collective-permute-done.7.refs_7_
  62.1 4.3 %collective-permute-done.5.refs_5_ = f32[64,512]{1,0:T(8,128)S(1)} collective-permute-done((f32[64,512]{1,0:T(8,128)S(1)}, f32[64,512]{1,0:T(8,128)S(1)}, u32[]{:S(2)}, u32[]{:S(2)}) %collective-permute-start.5) | collective-permute-done | bytes 131104 | tf_op jit(solution)/shard_map/ppermute | solution.py:457
  66.4 1.0 collective-permute-done.3.refs_3_
  68.2 2.9 chunk.1
  71.1 1.1 slice.136
  72.2 2.4 collective-permute-start.11
  74.6 1.3 collective-permute-start.10
  75.9 1.9 collective-permute-start.9
  77.9 1.6 collective-permute-done.10
  79.5 2.1 collective-permute-done.9
  81.7 1.0 select_select_fusion.1
  82.6 2.0 pad_maximum_fusion
  84.6 1.1 slice_bitcast_fusion
  85.8 2.2 collective-permute-start.12
  89.2 1.4 compare_select_fusion.live_ref
  90.6 19.4 %collective-permute-done.12.second_ref = f32[64,4096]{1,0:T(8,128)S(1)} collective-permute-done((f32[64,4096]{1,0:T(8,128)}, f32[64,4096]{1,0:T(8,128)S(1)}, u32[]{:S(2)}, u32[]{:S(2)}) %collective-permute-start.12) | collective-permute-done | bytes 1048608 | tf_op jit(solution)/shard_map/ppermute | solution.py:517
  110.1 6.1 %widen.1 = f32[16,128,512]{2,1,0:T(8,128)S(1)} custom-call(s32[2,64]{1,0:T(2,128)S(1)} %pad_add_fusion.list_ref, s32[2]{0:T(128)S(1)} %compare_select_fusion.live_ref, f32[64,4096]{1,0:T(8,128)S(1)} %get-tuple-element.24.first_ref, f32[64,4096]{1,0:T(8,128)S(1)} %collective-permute-done.12.second_ref), custom_call_target="tpu_custom_call" | custom-call | flops 8000000000 | bytes 6291456 | tf_op jit(solution)/shard_map/widen/pallas_call | solution.py:59
  116.2 1.9 copy-done
  118.1 45.3 %all-gather.2.cloned.1.call-done.square_ref.left_ref = f32[1024,3072]{1,0:T(8,128)} async-done(((f32[64,3072]{1,0:T(8,128)}), f32[1024,3072]{1,0:T(8,128)}) %all-gather.2.cloned.1.call-update) | async-done | bytes 12582928 | tf_op jit(solution)/shard_map/all_gather | solution.py:515
  163.4 1.8 constant_dynamic-slice_fusion.refs_0_
  165.1 2.0 collective-permute-start.15
  167.1 2.1 collective-permute-start.14
  169.2 1.3 collective-permute-start.13
  170.5 11.1 %all-to-all-start.1 = ((f32[16,128,512]{2,1,0:T(8,128)}), f32[16,128,512]{2,1,0:T(8,128)}, u32[]{:S(2)}, u32[]{:S(2)}) async-start(f32[16,128,512]{2,1,0:T(8,128)} %copy-done), calls=%async_computation.1 | async-start | bytes 8388608 | tf_op jit(solution)/shard_map/all_to_all | solution.py:437
  181.6 76.9 %inverse_factor.1.inv_ref = f32[1024,1024]{1,0:T(8,128)} custom-call(f32[1024,3072]{1,0:T(8,128)} %all-gather.2.cloned.1.call-done.square_ref.left_ref), custom_call_target="tpu_custom_call" | custom-call | flops 70000001024 | bytes 8388608 | tf_op jit(solution)/shard_map/inverse_factor/pallas_call | solution.py:267
  258.4 22.1 %finish.1.part_ref = f32[2048,512]{1,0:T(8,128)} custom-call(s32[2]{0:T(128)S(1)} %copy-done.5, f32[2048,512]{1,0:T(8,128)S(1)} %bitcast.98, f32[1024,3072]{1,0:T(8,128)} %all-gather.2.cloned.1.call-done.square_ref.left_ref, f32[1024,1024]{1,0:T(8,128)} %inverse_factor.1.inv_ref, f32[1024,512]{1,0:T(8,128)S(1)} %constant_dynamic-slice_fusion.refs_0_, ...), custom_call_target="tpu_custom_call" | custom-call | flops 22000001024 | bytes 27262976 | tf_op jit(solution)/shard_map/finish/pallas_call | solution.py:373
  280.6 6.8 %land.1 = f32[2048,512]{1,0:T(8,128)} custom-call(s32[2,16]{1,0:T(2,128)S(1)} %copy-done.4, s32[2]{0:T(128)S(1)} %copy-done.5, f32[2048,512]{1,0:T(8,128)} %finish.1.part_ref, f32[16,128,512]{2,1,0:T(8,128)} %all-to-all-done.1.source_ref), custom_call_target="tpu_custom_call", output_to_operand_aliasing={{}: (2, {})} | custom-call | flops 5000000000 | bytes 12582912 | tf_op jit(solution)/shard_map/land/pallas_call | solution.py:418
  (53 shorter events, 5.3 us)
Async XLA Ops:
  8.1 1.6 copy-start.1
  12.7 0.7 copy-start.6
  13.5 0.7 copy-start.7
  16.5 23.4 %all-to-all-start = ((f32[16,2,32,128]{3,2,1,0:T(8,128)}), f32[16,2,32,128]{3,2,1,0:T(8,128)S(1)}, u32[]{:S(2)}, u32[]{:S(2)}) async-start(f32[16,2,32,128]{3,2,1,0:T(8,128)} %turn.1), calls=%async_computation | async-start | bytes 1048576 | tf_op jit(solution)/shard_map/all_to_all | solution.py:437
  24.5 138.9 %all-gather.2.cloned.1.call-start = ((), (), s32[]{:S(2)}) async-start(), calls=%async_computation.2 | async-start | bytes 13369344 | tf_op jit(solution)/shard_map/all_gather | solution.py:515
  25.9 16.0 %collective-permute-start.6 = (f32[64,512]{1,0:T(8,128)S(1)}, f32[64,512]{1,0:T(8,128)S(1)}, u32[]{:S(2)}, u32[]{:S(2)}) collective-permute-start(f32[64,512]{1,0:T(8,128)S(1)} %get-tuple-element.19), channel_id=1, source_target_pairs={{0,12},{1,28},{2,44},{3,60},{4,0},{5,16},{6,32},{7,48},{8,4},{9,20... | collective-permute-start | bytes 393224 | tf_op jit(solution)/shard_map/ppermute | solution.py:457
  30.1 19.9 %collective-permute-start.4 = (f32[64,512]{1,0:T(8,128)S(1)}, f32[64,512]{1,0:T(8,128)S(1)}, u32[]{:S(2)}, u32[]{:S(2)}) collective-permute-start(f32[64,512]{1,0:T(8,128)S(1)} %get-tuple-element.20), channel_id=1, source_target_pairs={{0,8},{1,24},{2,40},{3,56},{4,12},{5,28},{6,44},{7,60},{8,0},{9,16... | collective-permute-start | bytes 393224 | tf_op jit(solution)/shard_map/ppermute | solution.py:457
  33.9 19.2 %collective-permute-start.2 = (f32[64,512]{1,0:T(8,128)S(1)}, f32[64,512]{1,0:T(8,128)S(1)}, u32[]{:S(2)}, u32[]{:S(2)}) collective-permute-start(f32[64,512]{1,0:T(8,128)S(1)} %get-tuple-element.21), channel_id=1, source_target_pairs={{0,4},{1,20},{2,36},{3,52},{4,8},{5,24},{6,40},{7,56},{8,12},{9,28... | collective-permute-start | bytes 393224 | tf_op jit(solution)/shard_map/ppermute | solution.py:457
  35.2 19.8 %collective-permute-start.1 = (f32[64,512]{1,0:T(8,128)S(1)}, f32[64,512]{1,0:T(8,128)S(1)}, u32[]{:S(2)}, u32[]{:S(2)}) collective-permute-start(f32[64,512]{1,0:T(8,128)S(1)} %get-tuple-element.22), channel_id=1, source_target_pairs={{0,2},{1,18},{2,34},{3,50},{4,6},{5,22},{6,38},{7,54},{8,10},{9,26... | collective-permute-start | bytes 393224 | tf_op jit(solution)/shard_map/ppermute | solution.py:457
  40.7 26.7 %collective-permute-start.8 = (f32[16,32,128]{2,1,0:T(8,128)S(1)}, f32[16,32,128]{2,1,0:T(8,128)S(1)}, u32[]{:S(2)}, u32[]{:S(2)}) collective-permute-start(f32[16,32,128]{2,1,0:T(8,128)S(1)} %get-tuple-element.27), channel_id=1, source_target_pairs={{0,64},{64,0},{128,192},{192,128},{1,65},{65,1},{129,193},{193,129... | collective-permute-start | bytes 786440 | tf_op jit(solution)/shard_map/ppermute | solution.py:511
  42.0 25.5 %copy-start.10 = (f32[64,512]{1,0:T(8,128)}, f32[64,512]{1,0:T(8,128)S(1)}, u32[]{:S(2)}) copy-start(f32[64,512]{1,0:T(8,128)S(1)} %collective-permute-done.6.refs_6_) | copy-start | bytes 393220
  42.0 20.2 %collective-permute-start.7 = (f32[64,512]{1,0:T(8,128)S(1)}, f32[64,512]{1,0:T(8,128)S(1)}, u32[]{:S(2)}, u32[]{:S(2)}) collective-permute-start(f32[64,512]{1,0:T(8,128)S(1)} %get-tuple-element.15), channel_id=1, source_target_pairs={{0,14},{1,30},{2,46},{3,62},{4,2},{5,18},{6,34},{7,50},{8,6},{9,22... | collective-permute-start | bytes 393224 | tf_op jit(solution)/shard_map/ppermute | solution.py:457
  50.0 17.5 %copy-start.11 = (f32[64,512]{1,0:T(8,128)}, f32[64,512]{1,0:T(8,128)S(1)}, u32[]{:S(2)}) copy-start(f32[64,512]{1,0:T(8,128)S(1)} %collective-permute-done.4.refs_4_) | copy-start | bytes 393220
  50.0 16.4 %collective-permute-start.5 = (f32[64,512]{1,0:T(8,128)S(1)}, f32[64,512]{1,0:T(8,128)S(1)}, u32[]{:S(2)}, u32[]{:S(2)}) collective-permute-start(f32[64,512]{1,0:T(8,128)S(1)} %get-tuple-element.16), channel_id=1, source_target_pairs={{0,10},{1,26},{2,42},{3,58},{4,14},{5,30},{6,46},{7,62},{8,2},{9,1... | collective-permute-start | bytes 393224 | tf_op jit(solution)/shard_map/ppermute | solution.py:457
  53.2 14.3 %copy-start.12 = (f32[64,512]{1,0:T(8,128)}, f32[64,512]{1,0:T(8,128)S(1)}, u32[]{:S(2)}) copy-start(f32[64,512]{1,0:T(8,128)S(1)} %collective-permute-done.2.refs_2_) | copy-start | bytes 393220
  53.2 14.2 %collective-permute-start.3 = (f32[64,512]{1,0:T(8,128)S(1)}, f32[64,512]{1,0:T(8,128)S(1)}, u32[]{:S(2)}, u32[]{:S(2)}) collective-permute-start(f32[64,512]{1,0:T(8,128)S(1)} %get-tuple-element.17), channel_id=1, source_target_pairs={{0,6},{1,22},{2,38},{3,54},{4,10},{5,26},{6,42},{7,58},{8,14},{9,3... | collective-permute-start | bytes 393224 | tf_op jit(solution)/shard_map/ppermute | solution.py:457
  55.1 12.4 %copy-start.13 = (f32[64,512]{1,0:T(8,128)}, f32[64,512]{1,0:T(8,128)S(1)}, u32[]{:S(2)}) copy-start(f32[64,512]{1,0:T(8,128)S(1)} %collective-permute-done.1.refs_1_) | copy-start | bytes 393220
  55.1 12.3 %collective-permute-start = (f32[64,512]{1,0:T(8,128)S(1)}, f32[64,512]{1,0:T(8,128)S(1)}, u32[]{:S(2)}, u32[]{:S(2)}) collective-permute-start(f32[64,512]{1,0:T(8,128)S(1)} %get-tuple-element.18), channel_id=1, source_target_pairs={{0,0},{1,16},{2,32},{3,48},{4,4},{5,20},{6,36},{7,52},{8,8},{9,24}... | collective-permute-start | bytes 393224 | tf_op jit(solution)/shard_map/ppermute | solution.py:457
  62.1 5.3 %copy-start.14 = (f32[64,512]{1,0:T(8,128)}, f32[64,512]{1,0:T(8,128)S(1)}, u32[]{:S(2)}) copy-start(f32[64,512]{1,0:T(8,128)S(1)} %collective-permute-done.7.refs_7_) | copy-start | bytes 393220
  66.4 1.1 copy-start.15
  67.4 0.7 copy-start.16
  67.4 0.7 copy-start.17
  67.4 0.8 copy-start.9
  71.1 13.5 %copy-start.2 = (f32[1,2,64,4096]{3,2,1,0:T(8,128)S(1)}, f32[1,2,64,4096]{3,2,1,0:T(8,128)}, u32[]{:S(2)}) copy-start(f32[1,2,64,4096]{3,2,1,0:T(8,128)} %param.5) | copy-start | bytes 6291460
  71.1 16.9 %copy-start.8 = (s32[4,2]{0,1:T(2,128)S(1)}, s32[4,2]{0,1:T(2,128)}, u32[]{:S(2)}) copy-start(s32[4,2]{0,1:T(2,128)} %param.7) | copy-start | bytes 100
  72.2 5.7 %collective-permute-start.11 = (f32[64,512]{1,0:T(8,128)S(1)}, f32[64,512]{1,0:T(8,128)S(1)}, u32[]{:S(2)}, u32[]{:S(2)}) collective-permute-start(f32[64,512]{1,0:T(8,128)S(1)} %slice.136), channel_id=1, source_target_pairs={{0,16},{16,32},{1,17},{17,33},{2,18},{18,34},{3,19},{19,35},{4,20}... | collective-permute-start | bytes 393224 | tf_op jit(solution)/shard_map/ppermute | solution.py:478
  74.6 4.9 %collective-permute-start.10 = (f32[64,512]{1,0:T(8,128)S(1)}, f32[64,512]{1,0:T(8,128)S(1)}, u32[]{:S(2)}, u32[]{:S(2)}) collective-permute-start(f32[64,512]{1,0:T(8,128)S(1)} %slice.136), channel_id=1, source_target_pairs={{0,32},{16,48},{1,33},{17,49},{2,34},{18,50},{3,35},{19,51},{4,36}... | collective-permute-start | bytes 393224 | tf_op jit(solution)/shard_map/ppermute | solution.py:478
  75.9 5.7 %collective-permute-start.9 = (f32[64,512]{1,0:T(8,128)S(1)}, f32[64,512]{1,0:T(8,128)S(1)}, u32[]{:S(2)}, u32[]{:S(2)}) collective-permute-start(f32[64,512]{1,0:T(8,128)S(1)} %slice.136), channel_id=1, source_target_pairs={{0,48},{16,0},{1,49},{17,1},{2,50},{18,2},{3,51},{19,3},{4,52},{20... | collective-permute-start | bytes 393224 | tf_op jit(solution)/shard_map/ppermute | solution.py:478
  85.8 24.3 %collective-permute-start.12 = (f32[64,4096]{1,0:T(8,128)}, f32[64,4096]{1,0:T(8,128)S(1)}, u32[]{:S(2)}, u32[]{:S(2)}) collective-permute-start(f32[64,4096]{1,0:T(8,128)} %get-tuple-element.23), channel_id=1, source_target_pairs={{0,64},{64,0},{128,192},{192,128},{1,65},{65,1},{129,193},{193,129... | collective-permute-start | bytes 3145736 | tf_op jit(solution)/shard_map/ppermute | solution.py:517
  116.2 1.9 copy-start
  165.1 93.3 %collective-permute-start.15 = (f32[1024,512]{1,0:T(8,128)S(1)}, f32[1024,512]{1,0:T(8,128)}, u32[]{:S(2)}, u32[]{:S(2)}) collective-permute-start(f32[1024,512]{1,0:T(8,128)S(1)} %constant_dynamic-slice_fusion.refs_0_), channel_id=1, source_target_pairs={{0,48},{17,1},{34,18},{51,35},{4,52},{21,5},{38,22},{55,39},{8,56}... | collective-permute-start | bytes 6291464 | tf_op jit(solution)/shard_map/ppermute | solution.py:468
  167.1 91.3 %collective-permute-start.14 = (f32[1024,512]{1,0:T(8,128)S(1)}, f32[1024,512]{1,0:T(8,128)}, u32[]{:S(2)}, u32[]{:S(2)}) collective-permute-start(f32[1024,512]{1,0:T(8,128)S(1)} %constant_dynamic-slice_fusion.refs_0_), channel_id=1, source_target_pairs={{0,32},{17,49},{34,2},{51,19},{4,36},{21,53},{38,6},{55,23},{8,40}... | collective-permute-start | bytes 6291464 | tf_op jit(solution)/shard_map/ppermute | solution.py:468
  169.2 89.2 %collective-permute-start.13 = (f32[1024,512]{1,0:T(8,128)S(1)}, f32[1024,512]{1,0:T(8,128)}, u32[]{:S(2)}, u32[]{:S(2)}) collective-permute-start(f32[1024,512]{1,0:T(8,128)S(1)} %constant_dynamic-slice_fusion.refs_0_), channel_id=1, source_target_pairs={{0,16},{17,33},{34,50},{51,3},{4,20},{21,37},{38,54},{55,7},{8,24}... | collective-permute-start | bytes 6291464 | tf_op jit(solution)/shard_map/ppermute | solution.py:468
  170.5 110.1 %all-to-all-start.1 = ((f32[16,128,512]{2,1,0:T(8,128)}), f32[16,128,512]{2,1,0:T(8,128)}, u32[]{:S(2)}, u32[]{:S(2)}) async-start(f32[16,128,512]{2,1,0:T(8,128)} %copy-done), calls=%async_computation.1 | async-start | bytes 8388608 | tf_op jit(solution)/shard_map/all_to_all | solution.py:437
  181.5 76.9 %copy-start.3 = (f32[1,2048,512]{2,1,0:T(8,128)S(1)}, f32[1,2048,512]{2,1,0:T(8,128)}, u32[]{:S(2)}) copy-start(f32[1,2048,512]{2,1,0:T(8,128)} %param.4) | copy-start | bytes 12582916
  181.5 76.9 %copy-start.5 = (s32[2]{0:T(128)S(1)}, s32[2]{0:T(128)}, u32[]{:S(2)}) copy-start(s32[2]{0:T(128)} %pad_add_fusion.1.place_ref) | copy-start | bytes 28
  258.4 22.1 %copy-start.4 = (s32[2,16]{1,0:T(2,128)S(1)}, s32[2,16]{1,0:T(2,128)}, u32[]{:S(2)}) copy-start(s32[2,16]{1,0:T(2,128)} %constant_dynamic-slice_fusion.2.target_ref) | copy-start | bytes 388
Sparse Core Ops, SparseCore 0:
  84.7 78.5 all-gather.1

commit v3 on v2

--- a/solution.py
+++ b/solution.py
@@ -67,47 +67,32 @@
     )(lists, live, first, second)
 
 
-def pick_kernel(list_ref, live_ref, rows_ref, first_ref, second_ref):
+def pivot_block(owner):
+    return owner % PANELS * PER_PANEL + owner // PANELS
+
+
+def pick_kernel(list_ref, live_ref, rows_ref, out_ref, picked_ref):
+    half = SBLK // 2
     lane = lax.broadcasted_iota(jnp.int32, (SBLK, TILE), 1)
-    for child, out_ref in enumerate((first_ref, second_ref)):
-        out_ref[...] = jnp.zeros_like(out_ref)
+    for child in range(2):
+        picked_ref[...] = jnp.zeros_like(picked_ref)
         for pair in range(rows_ref.shape[2] // TILE):
             both = rows_ref[child, :, pair * TILE : (pair + 1) * TILE]
             other = pltpu.roll(both, SBLK, 1)
-            for half in range(2):
-                block = pair * 2 + half
+            for part in range(2):
+                block = pair * 2 + part
                 target = list_ref[child, block]
 
                 @pl.when((target < PANELS * PER_PANEL) & (block < live_ref[child]))
                 def _():
                     parity = target % 2
-                    moved = jnp.where(parity == half, both, other)
+                    moved = jnp.where(parity == part, both, other)
                     spot = pl.ds(pl.multiple_of(target // 2 * TILE, TILE), TILE)
-                    out_ref[:, spot] = jnp.where(lane // SBLK == parity, moved, out_ref[:, spot])
-
-
-def pick(lists, live, rows):
-    width = PANELS * CR // 4
-    return pl.pallas_call(
-        pick_kernel,
-        grid=(1,),
-        out_shape=[jax.ShapeDtypeStruct((SBLK, PIVOTS), jnp.float32)] * 2,
-        in_specs=[smem_spec(), smem_spec(), pl.BlockSpec((2, SBLK, width), lambda i: (0, 0, 0))],
-        out_specs=[pl.BlockSpec((SBLK, PIVOTS), lambda i: (0, 0))] * 2,
-        compiler_params=pltpu.CompilerParams(vmem_limit_bytes=16 << 20),
-        cost_estimate=cost(3e-6, 2 << 20),
-        name="pick",
-    )(lists, live, rows)
-
-
-def pivot_block(owner):
-    return owner % PANELS * PER_PANEL + owner // PANELS
-
-
-def turn_kernel(first_ref, second_ref, out_ref):
-    half = SBLK // 2
-    for child, source in enumerate((first_ref, second_ref)):
-        turned = source[...].T
+                    picked_ref[:, spot] = jnp.where(
+                        lane // SBLK == parity, moved, picked_ref[:, spot]
+                    )
+
+        turned = picked_ref[...].T
         for owner in range(out_ref.shape[0]):
             at = pivot_block(owner) * SBLK
             out_ref[owner, child] = jnp.concatenate(
@@ -115,29 +100,35 @@
             )
 
 
-def turn(first, second):
+def pick(lists, live, rows):
+    width = PANELS * CR // 4
     owners = PIVOTS // SBLK
+    shape = (owners, 2, SBLK // 2, 2 * SBLK)
     return pl.pallas_call(
-        turn_kernel,
-        out_shape=jax.ShapeDtypeStruct((owners, 2, SBLK // 2, 2 * SBLK), jnp.float32),
-        in_specs=[vmem_spec()] * 2,
-        out_specs=vmem_spec(),
-        cost_estimate=cost(2e-6, 1 << 20),
-        name="turn",
-    )(first, second)
+        pick_kernel,
+        grid=(1,),
+        out_shape=jax.ShapeDtypeStruct(shape, jnp.float32),
+        in_specs=[smem_spec(), smem_spec(), pl.BlockSpec((2, SBLK, width), lambda i: (0, 0, 0))],
+        out_specs=pl.BlockSpec(shape, lambda i: (0, 0, 0, 0)),
+        scratch_shapes=[pltpu.VMEM((SBLK, PIVOTS), jnp.float32)],
+        compiler_params=pltpu.CompilerParams(vmem_limit_bytes=16 << 20),
+        cost_estimate=cost(5e-6, 2 << 20),
+        name="pick",
+    )(lists, live, rows)
 
 
 def chunk_kernel(target_ref, place_ref, *refs):
-    base_refs, first_ref, second_ref, out_ref = refs[:-3], refs[-3], refs[-2], refs[-1]
+    base_refs, (first_ref, second_ref, out_ref, head_ref) = refs[:-4], refs[-4:]
     steps = len(base_refs)
     half = SBLK // 2
     own_piece = place_ref[1] // PANELS
-    for slot in range(out_ref.shape[1] // B):
+    for slot in range(out_ref.shape[1] // B - PANELS):
+        at = slice((slot + PANELS) * B, (slot + PANELS + 1) * B)
         for step in range(steps):
 
             @pl.when((step + 2 * slot) % steps == own_piece)
             def _():
-                out_ref[:, slot * B : (slot + 1) * B] = base_refs[step][...]
+                out_ref[:, at] = base_refs[step][...]
 
     lane = lax.broadcasted_iota(jnp.int32, (half, TILE), 1)
     for child, source in enumerate((first_ref, second_ref)):
@@ -146,21 +137,27 @@
             other = pltpu.roll(both, SBLK, 1)
             target = target_ref[child, t]
             parity = target % 2
-            offset = target // (PER_PANEL * 4) * B + target % PER_PANEL // 2 * TILE
+            slot = target // (PER_PANEL * 4) + PANELS
+            offset = slot * B + target % PER_PANEL // 2 * TILE
             spot = pl.ds(pl.multiple_of(offset, TILE), TILE)
             keep = lane // SBLK == parity
             for part in range(2):
                 rows = slice(part * half, (part + 1) * half)
                 moved = jnp.where(parity == part, both, other)
                 out_ref[rows, spot] = out_ref[rows, spot] + jnp.where(keep, moved, 0.0)
+    head_ref[...] = out_ref[:, PANELS * B : (PANELS + 1) * B]
+    out_ref[:, : PANELS * B] = jnp.zeros((SBLK, PANELS * B), jnp.float32)
 
 
 def chunk(targets, place, base, first, second, width):
     return pl.pallas_call(
         chunk_kernel,
-        out_shape=jax.ShapeDtypeStruct((SBLK, width), jnp.float32),
+        out_shape=[
+            jax.ShapeDtypeStruct((SBLK, PIVOTS + width), jnp.float32),
+            jax.ShapeDtypeStruct((SBLK, B), jnp.float32),
+        ],
         in_specs=[smem_spec(), smem_spec()] + [vmem_spec()] * (len(base) + 2),
-        out_specs=vmem_spec(),
+        out_specs=[vmem_spec()] * 2,
         cost_estimate=cost(3e-6, 2 << 20),
         name="chunk",
     )(targets, place, *base, first, second)
@@ -224,62 +221,75 @@
     return jnp.concatenate(done, axis=0)
 
 
-def inverse_factor_kernel(square_ref, inv_ref, row_ref):
+def split(value):
+    high = value.astype(jnp.bfloat16)
+    return high, (value - high.astype(jnp.float32)).astype(jnp.bfloat16)
+
+
+def product(left, right, left_dim):
+    def part(first, second):
+        return lax.dot_general(
+            first, second, (((left_dim,), (0,)), ((), ())), preferred_element_type=jnp.float32
+        )
+
+    return part(left[0], right[0]) + (part(left[1], right[0]) + part(left[0], right[1]))
+
+
+def inverse_factor_kernel(
+    square_ref, high_ref, low_ref, full_ref, row_ref, upper_high_ref, upper_low_ref
+):
     for owner in range(PIVOTS // SBLK):
         at = pivot_block(owner) * SBLK
-        inv_ref[at : at + SBLK, :] = square_ref[owner * SBLK : (owner + 1) * SBLK, :]
-    lane = lax.broadcasted_iota(jnp.int32, (TILE, TILE), 1)
-    sub = lax.broadcasted_iota(jnp.int32, (TILE, TILE), 0)
-    identity = jnp.where(lane == sub, 1.0, 0.0)
+        full_ref[at : at + SBLK, :] = square_ref[owner * SBLK : (owner + 1) * SBLK, :]
+    lane = lax.broadcasted_iota(jnp.int32, (TILE, PIVOTS), 1)
     steps = PIVOTS // TILE
 
     def step(k, carry):
         at = pl.ds(pl.multiple_of(k * TILE, TILE), TILE)
-        inv_tile = inverse_factor_tile(inv_ref[at, at])
-        inv_ref[at, at] = identity
-        row_ref[...] = jnp.dot(
-            inv_tile, inv_ref[at, :], precision=HIGHEST, preferred_element_type=jnp.float32
-        )
-        inv_ref[at, :] = row_ref[...]
-
-        def below(i, carry):
-            rows = pl.ds(pl.multiple_of(i * TILE, TILE), TILE)
-            left = row_ref[:, rows]
-            inv_ref[rows, at] = jnp.zeros((TILE, TILE), jnp.float32)
-            inv_ref[rows, :] = inv_ref[rows, :] - lax.dot_general(
-                left,
-                row_ref[...],
-                (((0,), (0,)), ((), ())),
-                precision=HIGHEST,
-                preferred_element_type=jnp.float32,
-            )
-            return carry
-
-        return lax.fori_loop(k + 1, steps, below, carry)
+
+        @pl.when(k == 0)
+        def _():
+            row_ref[...] = full_ref[:TILE, :]
+
+        for block in range(1, steps):
+
+            @pl.when(k == block)
+            def _():
+                start = block * TILE
+                own = slice(start, start + TILE)
+                left = (upper_high_ref[:start, own], upper_low_ref[:start, own])
+                right = (upper_high_ref[:start, start:], upper_low_ref[:start, start:])
+                row_ref[:, start:] = full_ref[own, start:] - product(left, right, 0)
+                right = (high_ref[:start, :start], low_ref[:start, :start])
+                row_ref[:, :start] = -product(left, right, 0)
+
+        tile = inverse_factor_tile(row_ref[:, at])
+        row = product(split(tile), split(row_ref[...]), 1)
+        upper_high_ref[at, :], upper_low_ref[at, :] = split(row)
+        high_ref[at, :], low_ref[at, :] = split(jnp.where(lane < k * TILE, row, 0.0))
+        high_ref[at, at], low_ref[at, at] = split(tile)
+        return carry
 
     lax.fori_loop(0, steps, step, 0)
-    for k in range(steps - 1):
-        rows = slice(k * TILE, k * TILE + TILE)
-        inv_ref[rows, (k + 1) * TILE :] = jnp.zeros((TILE, PIVOTS - (k + 1) * TILE), jnp.float32)
 
 
 def inverse_factor(gathered):
     return pl.pallas_call(
         inverse_factor_kernel,
         grid=(1,),
-        out_shape=jax.ShapeDtypeStruct((PIVOTS, PIVOTS), jnp.float32),
+        out_shape=[jax.ShapeDtypeStruct((PIVOTS, PIVOTS), jnp.bfloat16)] * 2,
         in_specs=[pl.BlockSpec((PIVOTS, PIVOTS), lambda i: (0, 0))],
-        out_specs=pl.BlockSpec((PIVOTS, PIVOTS), lambda i: (0, 0)),
-        scratch_shapes=[pltpu.VMEM((TILE, PIVOTS), jnp.float32)],
-        compiler_params=pltpu.CompilerParams(vmem_limit_bytes=56 << 20),
-        cost_estimate=cost(70e-6, 8 << 20),
+        out_specs=[pl.BlockSpec((PIVOTS, PIVOTS), lambda i: (0, 0))] * 2,
+        scratch_shapes=[
+            pltpu.VMEM((PIVOTS, PIVOTS), jnp.float32),
+            pltpu.VMEM((TILE, PIVOTS), jnp.float32),
+            pltpu.VMEM((PIVOTS, PIVOTS), jnp.bfloat16),
+            pltpu.VMEM((PIVOTS, PIVOTS), jnp.bfloat16),
+        ],
+        compiler_params=pltpu.CompilerParams(vmem_limit_bytes=48 << 20),
+        cost_estimate=cost(65e-6, 8 << 20),
         name="inverse_factor",
     )(gathered)
-
-
-def split(value):
-    high = value.astype(jnp.bfloat16)
-    return high, (value - high.astype(jnp.float32)).astype(jnp.bfloat16)
 
 
 def keep_right(high_ref, low_ref, value, start, cols):
@@ -292,16 +302,9 @@
             low_ref[rows, cols] = low[at : at + SBLK]
 
 
-def from_left(left, right):
-    return lax.dot_general(
-        left, right, (((0,), (0,)), ((), ())), preferred_element_type=jnp.float32
-    )
-
-
-def finish_kernel(
-    place_ref, front_ref, left_ref, inv_ref, *refs
-):
-    above_refs, (out_ref, above_ref, solved_ref, high_ref, low_ref, sem) = refs[:-6], refs[-6:]
+def finish_kernel(place_ref, front_ref, left_ref, inv_high_ref, inv_low_ref, *refs):
+    above_refs = refs[:-7]
+    out_ref, above_ref, solved_high_ref, solved_low_ref, high_ref, low_ref, sem = refs[-7:]
     slot = pl.program_id(0)
     row_index, col_index = place_ref[0], place_ref[1]
     trailing = col_index >= PANELS
@@ -330,35 +333,31 @@
                 for copy in copies:
                     copy.wait()
 
+        above = split(above_ref[...])
         for i in range(PIVOTS // step):
             rows = slice(i * step, (i + 1) * step)
-            solved_ref[rows, :] = jnp.dot(
-                inv_ref[rows, : (i + 1) * step],
-                above_ref[: (i + 1) * step, :],
-                precision=HIGHEST,
-                preferred_element_type=jnp.float32,
+            end = (i + 1) * step
+            left = (inv_high_ref[rows, :end], inv_low_ref[rows, :end])
+            solved_high_ref[rows, :], solved_low_ref[rows, :] = split(
+                product(left, (above[0][:end], above[1][:end]), 1)
             )
         for j in range(PIVOTS // step):
             rows = slice(j * step, (j + 1) * step)
-            value = -lax.dot_general(
-                inv_ref[j * step :, rows],
-                solved_ref[j * step :, :],
-                (((0,), (0,)), ((), ())),
-                precision=HIGHEST,
-                preferred_element_type=jnp.float32,
-            )
-            keep_right(high_ref, low_ref, value, j * step, slice(None))
+            left = (inv_high_ref[j * step :, rows], inv_low_ref[j * step :, rows])
+            right = (solved_high_ref[j * step :, :], solved_low_ref[j * step :, :])
+            keep_right(high_ref, low_ref, -product(left, right, 0), j * step, slice(None))
 
     @pl.when((slot == 0) & jnp.logical_not(trailing))
     def _():
         for part in range(B // TILE):
             cols = slice(part * TILE, (part + 1) * TILE)
             own = pl.ds(pl.multiple_of(col_index * B + part * TILE, TILE), TILE)
-            keep_right(high_ref, low_ref, inv_ref[own, :].T, 0, cols)
-
-    left_high, left_low = split(left_ref[...])
-    total = from_left(left_low, high_ref[...]) + from_left(left_high, low_ref[...])
-    total = total + from_left(left_high, high_ref[...])
+            value = inv_high_ref[own, :].astype(jnp.float32) + inv_low_ref[own, :].astype(
+                jnp.float32
+            )
+            keep_right(high_ref, low_ref, value.T, 0, cols)
+
+    total = product(split(left_ref[...]), (high_ref[...], low_ref[...]), 0)
     out_ref[...] = total + jnp.where(trailing, front_ref[...], 0.0)
 
     @pl.when(slot == 0)
@@ -379,20 +378,17 @@
             pl.BlockSpec((B, B), lambda s: (s, 0)),
             pl.BlockSpec((PIVOTS, B), lambda s: (0, s + PANELS)),
             vmem_spec(),
+            vmem_spec(),
         ]
         + [pl.BlockSpec(memory_space=pl.ANY)] * len(above),
         out_specs=pl.BlockSpec((B, B), lambda s: (s, 0)),
-        scratch_shapes=[
-            pltpu.VMEM((PIVOTS, B), jnp.float32),
-            pltpu.VMEM((PIVOTS, B), jnp.float32),
-            pltpu.VMEM((PIVOTS, B), jnp.bfloat16),
-            pltpu.VMEM((PIVOTS, B), jnp.bfloat16),
-            pltpu.SemaphoreType.DMA((PIVOTS // SBLK,)),
-        ],
-        compiler_params=pltpu.CompilerParams(vmem_limit_bytes=40 << 20),
-        cost_estimate=cost(22e-6, 26 << 20),
+        scratch_shapes=[pltpu.VMEM((PIVOTS, B), jnp.float32)]
+        + [pltpu.VMEM((PIVOTS, B), jnp.bfloat16)] * 4
+        + [pltpu.SemaphoreType.DMA((PIVOTS // SBLK,))],
+        compiler_params=pltpu.CompilerParams(vmem_limit_bytes=30 << 20),
+        cost_estimate=cost(16e-6, 26 << 20),
         name="finish",
-    )(place, front, gathered, inverse, *above)
+    )(place, front, gathered, *inverse, *above)
 
 
 def land_kernel(target_ref, place_ref, part_ref, source_ref, out_ref):
@@ -506,12 +502,13 @@
     swap = [(cube, cube ^ 1) for cube in range(n_cube)]
 
     base = front_pieces(front[:B], n_row, n_col, col_index)
-    picked_first, picked_second = pick(own_lists, own_live, child_updates[0])
-    turned = exchange(turn(picked_first, picked_second))
+    packed = pick(own_lists, own_live, child_updates[0])
+    turned = exchange(packed)
     turned_second = lax.ppermute(turned[:, 1], "cube", swap)
-    own_chunk = chunk(targets, place, base, turned[:, 0], turned_second, front.shape[0])
-    heads = share_heads(own_chunk[:, :B], n_row, row_index)
-    own_chunk = jnp.concatenate(heads + [own_chunk], axis=1)
+    own_chunk, own_head = chunk(targets, place, base, turned[:, 0], turned_second, front.shape[0])
+    heads = share_heads(own_head, n_row, row_index)
+    for panel, head in enumerate(heads):
+        own_chunk = lax.dynamic_update_slice(own_chunk, head, (0, panel * B))
     gathered = lax.all_gather(own_chunk, "col", axis=0, tiled=True)
 
     arrived_child = lax.ppermute(child_updates[0, 1], "cube", swap)

time: 297 us -> 275 us (0.926)
  Pallas kernels: 120 us -> 98.5 us
  waiting for transfers between devices: 80.6 us -> 93 us
  starting transfers between devices: 56.8 us -> 48.5 us
  local copies, waits for them, and re-layouts: 15.2 us -> 11.6 us
    pallas_call x4 -> x3, Pallas kernels: 85.1 us -> 68.9 us  [the longest x1 61.3 us: inverse_factor(): pl.pallas_call(inverse_factor_kernel, grid=(1,), out_shape=[jax.ShapeDtyp...]
    all_to_all x2, waiting for transfers between devices: 0.01 us -> 10.5 us  [exchange(): return lax.all_to_all(value, 'col', split_axis=0, concat_axis=0, tiled=True)]
    all_to_all x2, starting transfers between devices: 19.1 us -> 13.2 us  [exchange(): return lax.all_to_all(value, 'col', split_axis=0, concat_axis=0, tiled=True)]
    pallas_call x1, Pallas kernels: 22.1 us -> 16.7 us  [finish(): pl.pallas_call(finish_kernel, grid=(slots,), out_shape=jax.ShapeDtypeStru...]
    dynamic_update_slice x0 -> x2, other arithmetic: none -> 3.2 us  [on_device(): own_chunk = lax.dynamic_update_slice(own_chunk, head, (0, panel * B))]
  transfers between devices with their start and end apart: 19 -> 19, of which waited for: 9 -> 10; matrix products, arithmetic and copies ran while one was open for 3% -> 4% of each run, Pallas kernels for 36% -> 31%
where the time goes in v3:
time: 275 us; the launch traced here: 273 us
  Pallas kernels  98.5 us (36%)
  waiting for transfers between devices  93 us (34%)
  starting transfers between devices  48.5 us (18%)
  between operations  13.8 us (5%)
  local copies, waits for them, and re-layouts  11.6 us (4%)
  other arithmetic  7.92 us (3%)
    pallas_call x1, Pallas kernels, inverse_factor(): pl.pallas_call(inverse_factor_kernel, grid=(1,), out_shape=[jax.ShapeDtyp...  61.3 us
    all_gather x1, waiting for transfers between devices, on_device(): gathered = lax.all_gather(own_chunk, 'col', axis=0, tiled=True)  47.2 us
    ppermute x8, starting transfers between devices, front_pieces(): received.append(lax.ppermute(value, ('row', 'col'), paths))  23 us
    ppermute x1, waiting for transfers between devices, on_device(): arrived_child = lax.ppermute(child_updates[0, 1], 'cube', swap)  19.1 us
    pallas_call x1, Pallas kernels, finish(): pl.pallas_call(finish_kernel, grid=(slots,), out_shape=jax.ShapeDtypeStru...  16.7 us
    all_to_all x2, starting transfers between devices, exchange(): return lax.all_to_all(value, 'col', split_axis=0, concat_axis=0, tiled=True)  13.2 us
    ppermute x8, waiting for transfers between devices, front_pieces(): received.append(lax.ppermute(value, ('row', 'col'), paths))  12.2 us
    all_to_all x2, waiting for transfers between devices, exchange(): return lax.all_to_all(value, 'col', split_axis=0, concat_axis=0, tiled=True)  10.5 us
  transfers between devices with their start and end apart: 19, of which 10 were waited for; matrix products, arithmetic and copies ran while one was open for 4% of the time, Pallas kernels for 31%

profile of v3, /device:TPU:97, one launch (start us, length us, event | category | flops | bytes accessed | tf_op | source)
XLA Modules:
  0.0 273.3 jit_solution(13590378343060175023)
XLA Ops:
  6.5 0.7 fusion.14.list_ref
  7.2 0.9 fusion.13
  8.1 1.6 copy-done.1
  9.7 4.4 %pick.1 = f32[16,2,32,128]{3,2,1,0:T(8,128)} custom-call(s32[2,64]{1,0:T(2,128)S(1)} %fusion.14.list_ref, s32[2]{0:T(128)S(1)} %compare_select_fusion.1.live_ref, f32[2,64,4096]{2,1,0:T(8,128)S(1)} %bitcast.97), custom_call_target="tpu_custom_call" | custom-call | flops 5000000000 | bytes 2097152 | tf_op jit(solution)/shard_map/pick/pallas_call | solution.py:107
  14.1 8.0 %all-to-all-start = ((f32[16,2,32,128]{3,2,1,0:T(8,128)}), f32[16,2,32,128]{3,2,1,0:T(8,128)S(1)}, u32[]{:S(2)}, u32[]{:S(2)}) async-start(f32[16,2,32,128]{3,2,1,0:T(8,128)} %pick.1), calls=%async_computation | async-start | bytes 1048576 | tf_op jit(solution)/shard_map/all_to_all | solution.py:433
  22.2 1.4 fusion.10
  23.6 4.0 %collective-permute-start.6 = (f32[64,512]{1,0:T(8,128)S(1)}, f32[64,512]{1,0:T(8,128)S(1)}, u32[]{:S(2)}, u32[]{:S(2)}) collective-permute-start(f32[64,512]{1,0:T(8,128)S(1)} %get-tuple-element.23), channel_id=1, source_target_pairs={{0,12},{1,28},{2,44},{3,60},{4,0},{5,16},{6,32},{7,48},{8,4},{9,20... | collective-permute-start | bytes 393224 | tf_op jit(solution)/shard_map/ppermute | solution.py:453
  27.6 3.9 %collective-permute-start.4 = (f32[64,512]{1,0:T(8,128)S(1)}, f32[64,512]{1,0:T(8,128)S(1)}, u32[]{:S(2)}, u32[]{:S(2)}) collective-permute-start(f32[64,512]{1,0:T(8,128)S(1)} %get-tuple-element.24), channel_id=1, source_target_pairs={{0,8},{1,24},{2,40},{3,56},{4,12},{5,28},{6,44},{7,60},{8,0},{9,16... | collective-permute-start | bytes 393224 | tf_op jit(solution)/shard_map/ppermute | solution.py:453
  31.4 1.3 collective-permute-start.2
  32.7 1.9 collective-permute-start.1
  34.7 0.7 constant_dynamic-slice_fusion.4
  35.4 0.7 fusion.12
  36.0 1.4 fusion.4
  37.4 0.7 slice_bitcast_fusion.2
  38.2 1.3 collective-permute-start.8
  39.5 3.7 %collective-permute-start.7 = (f32[64,512]{1,0:T(8,128)S(1)}, f32[64,512]{1,0:T(8,128)S(1)}, u32[]{:S(2)}, u32[]{:S(2)}) collective-permute-start(f32[64,512]{1,0:T(8,128)S(1)} %get-tuple-element.19), channel_id=1, source_target_pairs={{0,14},{1,30},{2,46},{3,62},{4,2},{5,18},{6,34},{7,50},{8,6},{9,22... | collective-permute-start | bytes 393224 | tf_op jit(solution)/shard_map/ppermute | solution.py:453
  43.3 4.4 %collective-permute-done.4.refs_4_ = f32[64,512]{1,0:T(8,128)S(1)} collective-permute-done((f32[64,512]{1,0:T(8,128)S(1)}, f32[64,512]{1,0:T(8,128)S(1)}, u32[]{:S(2)}, u32[]{:S(2)}) %collective-permute-start.4) | collective-permute-done | bytes 131104 | tf_op jit(solution)/shard_map/ppermute | solution.py:453
  47.6 1.9 collective-permute-start.5
  49.5 1.3 collective-permute-done.2.refs_2_
  50.8 1.9 collective-permute-start.3
  52.7 4.4 %collective-permute-start = (f32[64,512]{1,0:T(8,128)S(1)}, f32[64,512]{1,0:T(8,128)S(1)}, u32[]{:S(2)}, u32[]{:S(2)}) collective-permute-start(f32[64,512]{1,0:T(8,128)S(1)} %get-tuple-element.22), channel_id=1, source_target_pairs={{0,0},{1,16},{2,32},{3,48},{4,4},{5,20},{6,36},{7,52},{8,8},{9,24}... | collective-permute-start | bytes 393224 | tf_op jit(solution)/shard_map/ppermute | solution.py:453
  57.1 0.7 pad_add_fusion.1.place_ref
  58.4 1.0 collective-permute-done.7.refs_7_
  59.4 4.6 %collective-permute-done.5.refs_5_ = f32[64,512]{1,0:T(8,128)S(1)} collective-permute-done((f32[64,512]{1,0:T(8,128)S(1)}, f32[64,512]{1,0:T(8,128)S(1)}, u32[]{:S(2)}, u32[]{:S(2)}) %collective-permute-start.5) | collective-permute-done | bytes 131104 | tf_op jit(solution)/shard_map/ppermute | solution.py:453
  64.0 1.0 collective-permute-done.3.refs_3_
  65.8 3.2 %chunk.1 = (f32[64,3072]{1,0:T(8,128)}, f32[64,512]{1,0:T(8,128)}) custom-call(s32[2,16]{1,0:T(2,128)} %constant_dynamic-slice_fusion.2.target_ref, s32[2]{0:T(128)} %pad_add_fusion.1.place_ref, f32[64,512]{1,0:T(8,128)} %copy-done.15, f32[64,512]{1,0:T(8,128)} %copy-done.11, f32[64,512]{1,0:T(8,128)} %copy-done.10, f32[64,512]{1,0:T(8,128)} %copy-done.14, ...), custom_call_target="tpu_custom_call" | custom-call | flops 3000000000 | bytes 2097152 | tf_op jit(solution)/shard_map/chunk/pallas_call | solution.py:153
  69.0 2.6 collective-permute-start.11
  71.6 1.3 collective-permute-start.10
  72.9 1.9 collective-permute-start.9
  74.9 2.0 collective-permute-done.10
  76.9 1.9 collective-permute-done.9
  78.8 1.6 select_dynamic-update-slice_fusion.1
  80.4 1.6 select_dynamic-update-slice_fusion
  82.2 1.9 collective-permute-start.12
  85.2 1.3 compare_select_fusion.live_ref
  86.5 19.1 %collective-permute-done.12.second_ref = f32[64,4096]{1,0:T(8,128)S(1)} collective-permute-done((f32[64,4096]{1,0:T(8,128)S(1)}, f32[64,4096]{1,0:T(8,128)S(1)}, u32[]{:S(2)}, u32[]{:S(2)}) %collective-permute-start.12) | collective-permute-done | bytes 1048608 | tf_op jit(solution)/shard_map/ppermute | solution.py:514
  105.6 6.1 %widen.1 = f32[16,128,512]{2,1,0:T(8,128)S(1)} custom-call(s32[2,64]{1,0:T(2,128)S(1)} %pad_add_fusion.list_ref, s32[2]{0:T(128)S(1)} %compare_select_fusion.live_ref, f32[64,4096]{1,0:T(8,128)S(1)} %get-tuple-element.28.first_ref, f32[64,4096]{1,0:T(8,128)S(1)} %collective-permute-done.12.second_ref), custom_call_target="tpu_custom_call" | custom-call | flops 8000000000 | bytes 6291456 | tf_op jit(solution)/shard_map/widen/pallas_call | solution.py:59
  111.7 2.0 copy-done
  113.6 47.2 %all-gather.2.cloned.1.call-done.square_ref.left_ref = f32[1024,3072]{1,0:T(8,128)} async-done(((f32[64,3072]{1,0:T(8,128)}), f32[1024,3072]{1,0:T(8,128)}) %all-gather.2.cloned.1.call-update) | async-done | bytes 12582928 | tf_op jit(solution)/shard_map/all_gather | solution.py:512
  160.8 5.2 %all-to-all-start.1 = ((f32[16,128,512]{2,1,0:T(8,128)}), f32[16,128,512]{2,1,0:T(8,128)}, u32[]{:S(2)}, u32[]{:S(2)}) async-start(f32[16,128,512]{2,1,0:T(8,128)} %copy-done), calls=%async_computation.1 | async-start | bytes 8388608 | tf_op jit(solution)/shard_map/all_to_all | solution.py:433
  166.0 1.8 constant_dynamic-slice_fusion.refs_0_
  167.8 0.9 collective-permute-start.15
  168.7 0.9 collective-permute-start.14
  169.7 1.5 collective-permute-start.13
  171.1 61.3 %inverse_factor.1 = (bf16[1024,1024]{1,0:T(8,128)(2,1)S(1)}, bf16[1024,1024]{1,0:T(8,128)(2,1)S(1)}) custom-call(f32[1024,3072]{1,0:T(8,128)} %all-gather.2.cloned.1.call-done.square_ref.left_ref), custom_call_target="tpu_custom_call" | custom-call | flops 65000001536 | bytes 8388608 | tf_op jit(solution)/shard_map/inverse_factor/pallas_call | solution.py:277
  232.5 16.7 %finish.1.part_ref = f32[2048,512]{1,0:T(8,128)} custom-call(s32[2]{0:T(128)S(1)} %copy-done.5, f32[2048,512]{1,0:T(8,128)S(1)} %bitcast.98, f32[1024,3072]{1,0:T(8,128)} %all-gather.2.cloned.1.call-done.square_ref.left_ref, bf16[1024,1024]{1,0:T(8,128)(2,1)S(1)} %get-tuple-element.14.inv_high_ref, bf16[1024,1024]{1,0:T(8,128)(2,1)S(1)} %get-tuple-element.15.inv_low_ref, ...), custom_call_target="tpu_custom_call" | custom-call | flops 16000000000 | bytes 27262976 | tf_op jit(solution)/shard_map/finish/pallas_call | solution.py:372
  249.2 10.5 %all-to-all-done.1.source_ref = f32[16,128,512]{2,1,0:T(8,128)} async-done(((f32[16,128,512]{2,1,0:T(8,128)}), f32[16,128,512]{2,1,0:T(8,128)}, u32[]{:S(2)}, u32[]{:S(2)}) %all-to-all-start.1) | async-done | bytes 4194336 | tf_op jit(solution)/shard_map/all_to_all | solution.py:433
  259.7 6.7 %land.1 = f32[2048,512]{1,0:T(8,128)} custom-call(s32[2,16]{1,0:T(2,128)S(1)} %copy-done.4, s32[2]{0:T(128)S(1)} %copy-done.5, f32[2048,512]{1,0:T(8,128)} %finish.1.part_ref, f32[16,128,512]{2,1,0:T(8,128)} %all-to-all-done.1.source_ref), custom_call_target="tpu_custom_call", output_to_operand_aliasing={{}: (2, {})} | custom-call | flops 5000000000 | bytes 12582912 | tf_op jit(solution)/shard_map/land/pallas_call | solution.py:414
  (47 shorter events, 2.8 us)
Async XLA Ops:
  8.1 1.6 copy-start.1
  14.1 23.3 %all-to-all-start = ((f32[16,2,32,128]{3,2,1,0:T(8,128)}), f32[16,2,32,128]{3,2,1,0:T(8,128)S(1)}, u32[]{:S(2)}, u32[]{:S(2)}) async-start(f32[16,2,32,128]{3,2,1,0:T(8,128)} %pick.1), calls=%async_computation | async-start | bytes 1048576 | tf_op jit(solution)/shard_map/all_to_all | solution.py:433
  22.1 138.7 %all-gather.2.cloned.1.call-start = ((), (), s32[]{:S(2)}) async-start(), calls=%async_computation.2 | async-start | bytes 13369344 | tf_op jit(solution)/shard_map/all_gather | solution.py:512
  23.6 15.9 %collective-permute-start.6 = (f32[64,512]{1,0:T(8,128)S(1)}, f32[64,512]{1,0:T(8,128)S(1)}, u32[]{:S(2)}, u32[]{:S(2)}) collective-permute-start(f32[64,512]{1,0:T(8,128)S(1)} %get-tuple-element.23), channel_id=1, source_target_pairs={{0,12},{1,28},{2,44},{3,60},{4,0},{5,16},{6,32},{7,48},{8,4},{9,20... | collective-permute-start | bytes 393224 | tf_op jit(solution)/shard_map/ppermute | solution.py:453
  27.6 20.0 %collective-permute-start.4 = (f32[64,512]{1,0:T(8,128)S(1)}, f32[64,512]{1,0:T(8,128)S(1)}, u32[]{:S(2)}, u32[]{:S(2)}) collective-permute-start(f32[64,512]{1,0:T(8,128)S(1)} %get-tuple-element.24), channel_id=1, source_target_pairs={{0,8},{1,24},{2,40},{3,56},{4,12},{5,28},{6,44},{7,60},{8,0},{9,16... | collective-permute-start | bytes 393224 | tf_op jit(solution)/shard_map/ppermute | solution.py:453
  31.4 19.4 %collective-permute-start.2 = (f32[64,512]{1,0:T(8,128)S(1)}, f32[64,512]{1,0:T(8,128)S(1)}, u32[]{:S(2)}, u32[]{:S(2)}) collective-permute-start(f32[64,512]{1,0:T(8,128)S(1)} %get-tuple-element.25), channel_id=1, source_target_pairs={{0,4},{1,20},{2,36},{3,52},{4,8},{5,24},{6,40},{7,56},{8,12},{9,28... | collective-permute-start | bytes 393224 | tf_op jit(solution)/shard_map/ppermute | solution.py:453
  32.7 20.0 %collective-permute-start.1 = (f32[64,512]{1,0:T(8,128)S(1)}, f32[64,512]{1,0:T(8,128)S(1)}, u32[]{:S(2)}, u32[]{:S(2)}) collective-permute-start(f32[64,512]{1,0:T(8,128)S(1)} %get-tuple-element.26), channel_id=1, source_target_pairs={{0,2},{1,18},{2,34},{3,50},{4,6},{5,22},{6,38},{7,54},{8,10},{9,26... | collective-permute-start | bytes 393224 | tf_op jit(solution)/shard_map/ppermute | solution.py:453
  38.2 26.9 %collective-permute-start.8 = (f32[16,32,128]{2,1,0:T(8,128)S(1)}, f32[16,32,128]{2,1,0:T(8,128)S(1)}, u32[]{:S(2)}, u32[]{:S(2)}) collective-permute-start(f32[16,32,128]{2,1,0:T(8,128)S(1)} %get-tuple-element.29), channel_id=1, source_target_pairs={{0,64},{64,0},{128,192},{192,128},{1,65},{65,1},{129,193},{193,129... | collective-permute-start | bytes 786440 | tf_op jit(solution)/shard_map/ppermute | solution.py:507
  39.5 25.6 %copy-start.8 = (f32[64,512]{1,0:T(8,128)}, f32[64,512]{1,0:T(8,128)S(1)}, u32[]{:S(2)}) copy-start(f32[64,512]{1,0:T(8,128)S(1)} %collective-permute-done.6.refs_6_) | copy-start | bytes 393220
  39.5 19.9 %collective-permute-start.7 = (f32[64,512]{1,0:T(8,128)S(1)}, f32[64,512]{1,0:T(8,128)S(1)}, u32[]{:S(2)}, u32[]{:S(2)}) collective-permute-start(f32[64,512]{1,0:T(8,128)S(1)} %get-tuple-element.19), channel_id=1, source_target_pairs={{0,14},{1,30},{2,46},{3,62},{4,2},{5,18},{6,34},{7,50},{8,6},{9,22... | collective-permute-start | bytes 393224 | tf_op jit(solution)/shard_map/ppermute | solution.py:453
  47.6 17.5 %copy-start.9 = (f32[64,512]{1,0:T(8,128)}, f32[64,512]{1,0:T(8,128)S(1)}, u32[]{:S(2)}) copy-start(f32[64,512]{1,0:T(8,128)S(1)} %collective-permute-done.4.refs_4_) | copy-start | bytes 393220
  47.6 16.4 %collective-permute-start.5 = (f32[64,512]{1,0:T(8,128)S(1)}, f32[64,512]{1,0:T(8,128)S(1)}, u32[]{:S(2)}, u32[]{:S(2)}) collective-permute-start(f32[64,512]{1,0:T(8,128)S(1)} %get-tuple-element.20), channel_id=1, source_target_pairs={{0,10},{1,26},{2,42},{3,58},{4,14},{5,30},{6,46},{7,62},{8,2},{9,1... | collective-permute-start | bytes 393224 | tf_op jit(solution)/shard_map/ppermute | solution.py:453
  50.8 14.3 %copy-start.10 = (f32[64,512]{1,0:T(8,128)}, f32[64,512]{1,0:T(8,128)S(1)}, u32[]{:S(2)}) copy-start(f32[64,512]{1,0:T(8,128)S(1)} %collective-permute-done.2.refs_2_) | copy-start | bytes 393220
  50.8 14.2 %collective-permute-start.3 = (f32[64,512]{1,0:T(8,128)S(1)}, f32[64,512]{1,0:T(8,128)S(1)}, u32[]{:S(2)}, u32[]{:S(2)}) collective-permute-start(f32[64,512]{1,0:T(8,128)S(1)} %get-tuple-element.21), channel_id=1, source_target_pairs={{0,6},{1,22},{2,38},{3,54},{4,10},{5,26},{6,42},{7,58},{8,14},{9,3... | collective-permute-start | bytes 393224 | tf_op jit(solution)/shard_map/ppermute | solution.py:453
  52.7 12.4 %copy-start.11 = (f32[64,512]{1,0:T(8,128)}, f32[64,512]{1,0:T(8,128)S(1)}, u32[]{:S(2)}) copy-start(f32[64,512]{1,0:T(8,128)S(1)} %collective-permute-done.1.refs_1_) | copy-start | bytes 393220
  52.7 12.3 %collective-permute-start = (f32[64,512]{1,0:T(8,128)S(1)}, f32[64,512]{1,0:T(8,128)S(1)}, u32[]{:S(2)}, u32[]{:S(2)}) collective-permute-start(f32[64,512]{1,0:T(8,128)S(1)} %get-tuple-element.22), channel_id=1, source_target_pairs={{0,0},{1,16},{2,32},{3,48},{4,4},{5,20},{6,36},{7,52},{8,8},{9,24}... | collective-permute-start | bytes 393224 | tf_op jit(solution)/shard_map/ppermute | solution.py:453
  59.4 5.7 %copy-start.12 = (f32[64,512]{1,0:T(8,128)}, f32[64,512]{1,0:T(8,128)S(1)}, u32[]{:S(2)}) copy-start(f32[64,512]{1,0:T(8,128)S(1)} %collective-permute-done.7.refs_7_) | copy-start | bytes 393220
  64.0 1.1 copy-start.13
  65.0 0.7 copy-start.14
  65.0 0.7 copy-start.15
  65.0 0.8 copy-start.7
  65.8 16.2 %copy-start.2 = (f32[1,2,64,4096]{3,2,1,0:T(8,128)S(1)}, f32[1,2,64,4096]{3,2,1,0:T(8,128)}, u32[]{:S(2)}) copy-start(f32[1,2,64,4096]{3,2,1,0:T(8,128)} %param.5) | copy-start | bytes 6291460
  69.0 15.0 %copy-start.6 = (s32[4,2]{0,1:T(2,128)S(1)}, s32[4,2]{0,1:T(2,128)}, u32[]{:S(2)}) copy-start(s32[4,2]{0,1:T(2,128)} %param.7) | copy-start | bytes 100
  69.0 5.8 %collective-permute-start.11 = (f32[64,512]{1,0:T(8,128)}, f32[64,512]{1,0:T(8,128)S(1)}, u32[]{:S(2)}, u32[]{:S(2)}) collective-permute-start(f32[64,512]{1,0:T(8,128)} %get-tuple-element.12), channel_id=1, source_target_pairs={{0,16},{16,32},{1,17},{17,33},{2,18},{18,34},{3,19},{19,35},{4,20}... | collective-permute-start | bytes 393224 | tf_op jit(solution)/shard_map/ppermute | solution.py:474
  71.6 5.3 %collective-permute-start.10 = (f32[64,512]{1,0:T(8,128)}, f32[64,512]{1,0:T(8,128)S(1)}, u32[]{:S(2)}, u32[]{:S(2)}) collective-permute-start(f32[64,512]{1,0:T(8,128)} %get-tuple-element.12), channel_id=1, source_target_pairs={{0,32},{16,48},{1,33},{17,49},{2,34},{18,50},{3,35},{19,51},{4,36}... | collective-permute-start | bytes 393224 | tf_op jit(solution)/shard_map/ppermute | solution.py:474
  72.9 5.9 %collective-permute-start.9 = (f32[64,512]{1,0:T(8,128)}, f32[64,512]{1,0:T(8,128)S(1)}, u32[]{:S(2)}, u32[]{:S(2)}) collective-permute-start(f32[64,512]{1,0:T(8,128)} %get-tuple-element.12), channel_id=1, source_target_pairs={{0,48},{16,0},{1,49},{17,1},{2,50},{18,2},{3,51},{19,3},{4,52},{20... | collective-permute-start | bytes 393224 | tf_op jit(solution)/shard_map/ppermute | solution.py:474
  82.2 23.4 %collective-permute-start.12 = (f32[64,4096]{1,0:T(8,128)S(1)}, f32[64,4096]{1,0:T(8,128)S(1)}, u32[]{:S(2)}, u32[]{:S(2)}) collective-permute-start(f32[64,4096]{1,0:T(8,128)S(1)} %get-tuple-element.27), channel_id=1, source_target_pairs={{0,64},{64,0},{128,192},{192,128},{1,65},{65,1},{129,193},{193,129... | collective-permute-start | bytes 3145736 | tf_op jit(solution)/shard_map/ppermute | solution.py:514
  111.7 2.0 copy-start
  160.8 98.9 %all-to-all-start.1 = ((f32[16,128,512]{2,1,0:T(8,128)}), f32[16,128,512]{2,1,0:T(8,128)}, u32[]{:S(2)}, u32[]{:S(2)}) async-start(f32[16,128,512]{2,1,0:T(8,128)} %copy-done), calls=%async_computation.1 | async-start | bytes 8388608 | tf_op jit(solution)/shard_map/all_to_all | solution.py:433
  167.8 64.7 %copy-start.3 = (f32[1,2048,512]{2,1,0:T(8,128)S(1)}, f32[1,2048,512]{2,1,0:T(8,128)}, u32[]{:S(2)}) copy-start(f32[1,2048,512]{2,1,0:T(8,128)} %param.4) | copy-start | bytes 12582916
  167.8 64.7 %copy-start.5 = (s32[2]{0:T(128)S(1)}, s32[2]{0:T(128)}, u32[]{:S(2)}) copy-start(s32[2]{0:T(128)} %pad_add_fusion.1.place_ref) | copy-start | bytes 28
  167.8 64.6 %collective-permute-start.15 = (f32[1024,512]{1,0:T(8,128)S(1)}, f32[1024,512]{1,0:T(8,128)S(1)}, u32[]{:S(2)}, u32[]{:S(2)}) collective-permute-start(f32[1024,512]{1,0:T(8,128)S(1)} %constant_dynamic-slice_fusion.refs_0_), channel_id=1, source_target_pairs={{0,48},{17,1},{34,18},{51,35},{4,52},{21,5},{38,22},{55,39},{8,56}... | collective-permute-start | bytes 6291464 | tf_op jit(solution)/shard_map/ppermute | solution.py:464
  168.7 63.7 %collective-permute-start.14 = (f32[1024,512]{1,0:T(8,128)S(1)}, f32[1024,512]{1,0:T(8,128)S(1)}, u32[]{:S(2)}, u32[]{:S(2)}) collective-permute-start(f32[1024,512]{1,0:T(8,128)S(1)} %constant_dynamic-slice_fusion.refs_0_), channel_id=1, source_target_pairs={{0,32},{17,49},{34,2},{51,19},{4,36},{21,53},{38,6},{55,23},{8,40}... | collective-permute-start | bytes 6291464 | tf_op jit(solution)/shard_map/ppermute | solution.py:464
  169.7 62.8 %collective-permute-start.13 = (f32[1024,512]{1,0:T(8,128)S(1)}, f32[1024,512]{1,0:T(8,128)}, u32[]{:S(2)}, u32[]{:S(2)}) collective-permute-start(f32[1024,512]{1,0:T(8,128)S(1)} %constant_dynamic-slice_fusion.refs_0_), channel_id=1, source_target_pairs={{0,16},{17,33},{34,50},{51,3},{4,20},{21,37},{38,54},{55,7},{8,24}... | collective-permute-start | bytes 6291464 | tf_op jit(solution)/shard_map/ppermute | solution.py:464
  232.5 27.3 %copy-start.4 = (s32[2,16]{1,0:T(2,128)S(1)}, s32[2,16]{1,0:T(2,128)}, u32[]{:S(2)}) copy-start(s32[2,16]{1,0:T(2,128)} %constant_dynamic-slice_fusion.2.target_ref) | copy-start | bytes 388
Sparse Core Ops, SparseCore 0:
  82.2 78.6 all-gather.1

commit v4 on v3

--- a/solution.py
+++ b/solution.py
@@ -1,3 +1,5 @@
+import functools
+
 import jax
 import jax.numpy as jnp
 from jax import lax
@@ -31,14 +33,18 @@
     return pl.CostEstimate(flops=int(seconds * 1e15), bytes_accessed=moved, transcendentals=0)
 
 
-def widen_kernel(list_ref, live_ref, first_ref, second_ref, out_ref):
+def widen_kernel(parts, list_ref, live_ref, *refs):
+    out_ref = refs[-1]
     out_ref[...] = jnp.zeros_like(out_ref)
-    lane = lax.broadcasted_iota(jnp.int32, (SBLK, TILE), 1)
-    for child, rows_ref in enumerate((first_ref, second_ref)):
-        out_rows = slice(child * SBLK, (child + 1) * SBLK)
+    begin = 0
+    for (child, start, count), rows_ref in zip(parts, refs[:-1]):
+        lane = lax.broadcasted_iota(jnp.int32, (count, TILE), 1)
+        in_rows = slice(start, start + count)
+        out_rows = slice(begin, begin + count)
+        begin += count
 
         def place(pair, carry):
-            both = rows_ref[:, pl.ds(pl.multiple_of(pair * TILE, TILE), TILE)]
+            both = rows_ref[in_rows, pl.ds(pl.multiple_of(pair * TILE, TILE), TILE)]
             other = pltpu.roll(both, SBLK, 1)
             for half in range(2):
                 block = pair * 2 + half
@@ -55,16 +61,17 @@
         lax.fori_loop(0, CR // TILE, place, 0)
 
 
-def widen(lists, live, first, second):
+def widen(lists, live, parts, rows):
+    total = sum(count for _, _, count in parts)
     return pl.pallas_call(
-        widen_kernel,
-        out_shape=jax.ShapeDtypeStruct((F // B, 2 * SBLK, B), jnp.float32),
-        in_specs=[smem_spec(), smem_spec(), vmem_spec(), vmem_spec()],
+        functools.partial(widen_kernel, parts),
+        out_shape=jax.ShapeDtypeStruct((F // B, total, B), jnp.float32),
+        in_specs=[smem_spec(), smem_spec()] + [vmem_spec()] * len(rows),
         out_specs=vmem_spec(),
         compiler_params=pltpu.CompilerParams(vmem_limit_bytes=16 << 20),
-        cost_estimate=cost(8e-6, 6 << 20),
+        cost_estimate=cost(total * 6e-8, total * 50000),
         name="widen",
-    )(lists, live, first, second)
+    )(lists, live, *rows)
 
 
 def pivot_block(owner):
@@ -391,25 +398,32 @@
     )(place, front, gathered, *inverse, *above)
 
 
-def land_kernel(target_ref, place_ref, part_ref, source_ref, out_ref):
+def land_kernel(target_ref, place_ref, part_ref, early_ref, late_ref, out_ref):
     slot = pl.program_id(0)
     row_index, col_index = place_ref[0], place_ref[1]
+    early = early_ref.shape[1]
     out_ref[...] = part_ref[...]
 
     @pl.when((col_index >= PANELS) & (slot * 4 + row_index >= PANELS))
     def _():
-        for child in range(source_ref.shape[1] // SBLK):
-            for t in range(source_ref.shape[0]):
+        for child in range(2):
+            for t in range(late_ref.shape[0]):
                 target = target_ref[child, t]
 
                 @pl.when(target // (PER_PANEL * 4) == slot)
                 def _():
-                    rows = pl.ds(pl.multiple_of(target % PER_PANEL * SBLK, SBLK), SBLK)
-                    at = slice(child * SBLK, (child + 1) * SBLK)
-                    out_ref[rows, :] = out_ref[rows, :] + source_ref[t, at]
-
-
-def land(targets, place, part, source):
+                    begin = target % PER_PANEL * SBLK
+                    if child == 0:
+                        rows = pl.ds(pl.multiple_of(begin, SBLK), early)
+                        out_ref[rows, :] = out_ref[rows, :] + early_ref[t]
+                        rows = pl.ds(pl.multiple_of(begin + early, 8), SBLK - early)
+                        out_ref[rows, :] = out_ref[rows, :] + late_ref[t, : SBLK - early]
+                    else:
+                        rows = pl.ds(pl.multiple_of(begin, SBLK), SBLK)
+                        out_ref[rows, :] = out_ref[rows, :] + late_ref[t, SBLK - early :]
+
+
+def land(targets, place, part, early, late):
     slots = part.shape[0] // B
     return pl.pallas_call(
         land_kernel,
@@ -420,13 +434,14 @@
             smem_spec(),
             pl.BlockSpec((B, B), lambda s: (s, 0)),
             vmem_spec(),
+            vmem_spec(),
         ],
         out_specs=pl.BlockSpec((B, B), lambda s: (s, 0)),
         input_output_aliases={2: 0},
         compiler_params=pltpu.CompilerParams(vmem_limit_bytes=16 << 20),
         cost_estimate=cost(5e-6, 12 << 20),
         name="land",
-    )(targets, place, part, source)
+    )(targets, place, part, early, late)
 
 
 def exchange(value):
@@ -506,13 +521,19 @@
     turned = exchange(packed)
     turned_second = lax.ppermute(turned[:, 1], "cube", swap)
     own_chunk, own_head = chunk(targets, place, base, turned[:, 0], turned_second, front.shape[0])
+    early = SBLK // 2
+    own_rows = child_updates[0, 0]
+    spread_early = widen(block_lists, live, ((0, 0, early),), (own_rows,))
+    own_head, spread_early = lax.optimization_barrier((own_head, spread_early))
     heads = share_heads(own_head, n_row, row_index)
+    arrived_early = exchange(spread_early)
     for panel, head in enumerate(heads):
         own_chunk = lax.dynamic_update_slice(own_chunk, head, (0, panel * B))
     gathered = lax.all_gather(own_chunk, "col", axis=0, tiled=True)
 
     arrived_child = lax.ppermute(child_updates[0, 1], "cube", swap)
-    spread = widen(block_lists, live, child_updates[0, 0], arrived_child)
+    parts = ((0, early, SBLK - early), (1, 0, SBLK))
+    spread = widen(block_lists, live, parts, (own_rows, arrived_child))
     gathered, spread = lax.optimization_barrier((gathered, spread))
     arrived = exchange(spread)
 
@@ -522,7 +543,7 @@
     above = share_above(own_above, n_row, n_col)
     inverse = inverse_factor(gathered)
     part = finish(place, front, gathered, inverse, above)
-    return land(targets, place, part, arrived)[None]
+    return land(targets, place, part, arrived_early, arrived)[None]
 
 
 def solution(mesh):

time: 275 us -> 299 us (1.087)
  starting transfers between devices: 48.5 us -> 60.6 us
  Pallas kernels: 98.5 us -> 103 us
  local copies, waits for them, and re-layouts: 11.6 us -> 15.3 us
    all_to_all x2 -> x3, starting transfers between devices: 13.2 us -> 28.8 us  [exchange(): return lax.all_to_all(value, 'col', split_axis=0, concat_axis=0, tiled=True)]
    all_to_all x2 -> x3, waiting for transfers between devices: 10.5 us -> 0.01 us  [exchange(): return lax.all_to_all(value, 'col', split_axis=0, concat_axis=0, tiled=True)]
    all_gather x1, waiting for transfers between devices: 47.2 us -> 54.9 us  [on_device(): gathered = lax.all_gather(own_chunk, 'col', axis=0, tiled=True)]
    pallas_call x1 -> x2, Pallas kernels: 6.12 us -> 11.6 us  [widen(): pl.pallas_call(functools.partial(widen_kernel, parts), out_shape=jax.Shap...]
    ppermute x1, waiting for transfers between devices: 19.1 us -> 24.4 us  [on_device(): arrived_child = lax.ppermute(child_updates[0, 1], 'cube', swap)]
    ppermute x8, starting transfers between devices: 23 us -> 19.4 us  [front_pieces(): received.append(lax.ppermute(value, ('row', 'col'), paths))]
  transfers between devices with their start and end apart: 19 -> 20, of which waited for: 10 -> 6; matrix products, arithmetic and copies ran while one was open for 4% -> 5% of each run, Pallas kernels for 31% -> 30%
where the time goes in v4:
time: 299 us; the launch traced here: 297 us
  Pallas kernels  103 us (34%)
  waiting for transfers between devices  95.7 us (32%)
  starting transfers between devices  60.6 us (20%)
  local copies, waits for them, and re-layouts  15.3 us (5%)
  between operations  13.8 us (5%)
  other arithmetic  9.34 us (3%)
    pallas_call x1, Pallas kernels, inverse_factor(): pl.pallas_call(inverse_factor_kernel, grid=(1,), out_shape=[jax.ShapeDtyp...  61.4 us
    all_gather x1, waiting for transfers between devices, on_device(): gathered = lax.all_gather(own_chunk, 'col', axis=0, tiled=True)  54.9 us
    all_to_all x3, starting transfers between devices, exchange(): return lax.all_to_all(value, 'col', split_axis=0, concat_axis=0, tiled=True)  28.8 us
    ppermute x1, waiting for transfers between devices, on_device(): arrived_child = lax.ppermute(child_updates[0, 1], 'cube', swap)  24.4 us
    ppermute x8, starting transfers between devices, front_pieces(): received.append(lax.ppermute(value, ('row', 'col'), paths))  19.4 us
    pallas_call x1, Pallas kernels, finish(): pl.pallas_call(finish_kernel, grid=(slots,), out_shape=jax.ShapeDtypeStru...  16.7 us
    ppermute x8, waiting for transfers between devices, front_pieces(): received.append(lax.ppermute(value, ('row', 'col'), paths))  12.4 us
    pallas_call x2, Pallas kernels, widen(): pl.pallas_call(functools.partial(widen_kernel, parts), out_shape=jax.Shap...  11.6 us
  transfers between devices with their start and end apart: 20, of which 6 were waited for; matrix products, arithmetic and copies ran while one was open for 5% of the time, Pallas kernels for 30%

profile of v4, /device:TPU:97, one launch (start us, length us, event | category | flops | bytes accessed | tf_op | source)
XLA Modules:
  0.0 297.4 jit_solution(9929812895762218682)
XLA Ops:
  6.5 0.7 fusion.14.list_ref
  7.2 0.9 fusion.13
  8.1 1.6 copy-done
  9.7 4.5 %pick.1 = f32[16,2,32,128]{3,2,1,0:T(8,128)} custom-call(s32[2,64]{1,0:T(2,128)S(1)} %fusion.14.list_ref, s32[2]{0:T(128)S(1)} %compare_select_fusion.1.live_ref, f32[2,64,4096]{2,1,0:T(8,128)S(1)} %bitcast.97), custom_call_target="tpu_custom_call" | custom-call | flops 5000000000 | bytes 2097152 | tf_op jit(solution)/shard_map/pick/pallas_call | solution.py:114
  14.2 8.1 %all-to-all-start = ((f32[16,2,32,128]{3,2,1,0:T(8,128)}), f32[16,2,32,128]{3,2,1,0:T(8,128)}, u32[]{:S(2)}, u32[]{:S(2)}) async-start(f32[16,2,32,128]{3,2,1,0:T(8,128)} %pick.1), calls=%async_computation | async-start | bytes 1048576 | tf_op jit(solution)/shard_map/all_to_all | solution.py:448
  22.4 2.1 fusion.10
  24.5 4.8 %collective-permute-start.6 = (f32[64,512]{1,0:T(8,128)}, f32[64,512]{1,0:T(8,128)}, u32[]{:S(2)}, u32[]{:S(2)}) collective-permute-start(f32[64,512]{1,0:T(8,128)} %get-tuple-element.27), channel_id=1, source_target_pairs={{0,12},{1,28},{2,44},{3,60},{4,0},{5,16},{6,32},{7,48},{8,4},{9,20... | collective-permute-start | bytes 393224 | tf_op jit(solution)/shard_map/ppermute | solution.py:468
  29.2 3.8 %collective-permute-start.4 = (f32[64,512]{1,0:T(8,128)}, f32[64,512]{1,0:T(8,128)}, u32[]{:S(2)}, u32[]{:S(2)}) collective-permute-start(f32[64,512]{1,0:T(8,128)} %get-tuple-element.28), channel_id=1, source_target_pairs={{0,8},{1,24},{2,40},{3,56},{4,12},{5,28},{6,44},{7,60},{8,0},{9,16... | collective-permute-start | bytes 393224 | tf_op jit(solution)/shard_map/ppermute | solution.py:468
  33.0 1.9 collective-permute-start.2
  35.0 1.9 collective-permute-start.1
  36.9 0.7 constant_dynamic-slice_fusion.4
  37.6 2.1 fusion.4
  40.2 0.7 fusion.12
  41.5 1.4 compare_select_fusion.live_ref
  42.8 1.1 slice_bitcast_fusion
  44.0 1.8 slice_bitcast_fusion.2
  45.7 1.2 collective-permute-start.8
  46.9 4.1 %widen.2 = f32[16,32,512]{2,1,0:T(8,128)} custom-call(s32[2,64]{1,0:T(2,128)S(1)} %pad_add_fusion.list_ref, s32[2]{0:T(128)S(1)} %compare_select_fusion.live_ref, f32[64,4096]{1,0:T(8,128)S(1)} %get-tuple-element.32.refs_0_), custom_call_target="tpu_custom_call" | custom-call | flops 1920000000 | bytes 1600000 | tf_op jit(solution)/shard_map/widen/pallas_call | solution.py:66
  51.1 1.9 collective-permute-start.7
  53.0 1.9 collective-permute-start.5
  55.0 1.9 collective-permute-start.3
  56.9 1.3 collective-permute-start
  58.8 0.6 constant_dynamic-slice_fusion.2.target_ref
  59.3 7.9 %collective-permute-done.7.refs_7_ = f32[64,512]{1,0:T(8,128)S(1)} collective-permute-done((f32[64,512]{1,0:T(8,128)S(1)}, f32[64,512]{1,0:T(8,128)S(1)}, u32[]{:S(2)}, u32[]{:S(2)}) %collective-permute-start.7) | collective-permute-done | bytes 131104 | tf_op jit(solution)/shard_map/ppermute | solution.py:468
  67.3 4.5 %collective-permute-done.5.refs_5_ = f32[64,512]{1,0:T(8,128)S(1)} collective-permute-done((f32[64,512]{1,0:T(8,128)S(1)}, f32[64,512]{1,0:T(8,128)S(1)}, u32[]{:S(2)}, u32[]{:S(2)}) %collective-permute-start.5) | collective-permute-done | bytes 131104 | tf_op jit(solution)/shard_map/ppermute | solution.py:468
  71.8 0.6 copy-done.12
  72.6 3.1 %chunk.1 = (f32[64,3072]{1,0:T(8,128)}, f32[64,512]{1,0:T(8,128)}) custom-call(s32[2,16]{1,0:T(2,128)} %constant_dynamic-slice_fusion.2.target_ref, s32[2]{0:T(128)} %pad_add_fusion.1.place_ref, f32[64,512]{1,0:T(8,128)} %copy-done.14, f32[64,512]{1,0:T(8,128)} %collective-permute-done.1.refs_1_, f32[64,512]{1,0:T(8,128)} %collective-permute-done.2.refs_2_, ...), custom_call_target="tpu_custom_call" | custom-call | flops 3000000000 | bytes 2097152 | tf_op jit(solution)/shard_map/chunk/pallas_call | solution.py:160
  75.7 2.4 collective-permute-start.11
  78.0 1.3 collective-permute-start.10
  79.3 1.9 collective-permute-start.9
  81.3 0.8 collective-permute-done.10
  82.2 3.1 %collective-permute-done.9 = f32[64,512]{1,0:T(8,128)S(1)} collective-permute-done((f32[64,512]{1,0:T(8,128)}, f32[64,512]{1,0:T(8,128)S(1)}, u32[]{:S(2)}, u32[]{:S(2)}) %collective-permute-start.9) | collective-permute-done | bytes 131104 | tf_op jit(solution)/shard_map/ppermute | solution.py:489
  85.3 1.6 select_dynamic-update-slice_fusion.1
  86.9 1.6 select_dynamic-update-slice_fusion
  88.5 10.7 %all-to-all-start.1 = ((f32[16,32,512]{2,1,0:T(8,128)}), f32[16,32,512]{2,1,0:T(8,128)S(1)}, u32[]{:S(2)}, u32[]{:S(2)}) async-start(f32[16,32,512]{2,1,0:T(8,128)} %widen.2), calls=%async_computation.1 | async-start | bytes 2097152 | tf_op jit(solution)/shard_map/all_to_all | solution.py:448
  99.6 24.4 %collective-permute-done.12.refs_1_ = f32[64,4096]{1,0:T(8,128)S(1)} collective-permute-done((f32[64,4096]{1,0:T(8,128)}, f32[64,4096]{1,0:T(8,128)S(1)}, u32[]{:S(2)}, u32[]{:S(2)}) %collective-permute-start.12) | collective-permute-done | bytes 1048608 | tf_op jit(solution)/shard_map/ppermute | solution.py:534
  124.0 7.5 %widen.3 = f32[16,96,512]{2,1,0:T(8,128)} custom-call(s32[2,64]{1,0:T(2,128)S(1)} %pad_add_fusion.list_ref, s32[2]{0:T(128)S(1)} %compare_select_fusion.live_ref, f32[64,4096]{1,0:T(8,128)S(1)} %get-tuple-element.32.refs_0_, f32[64,4096]{1,0:T(8,128)S(1)} %collective-permute-done.12.refs_1_), custom_call_target="tpu_custom_call" | custom-call | flops 5760000000 | bytes 4800000 | tf_op jit(solution)/shard_map/widen/pallas_call | solution.py:66
  131.5 54.9 %all-gather.2.cloned.1.call-done.square_ref.left_ref = f32[1024,3072]{1,0:T(8,128)} async-done(((f32[64,3072]{1,0:T(8,128)}), f32[1024,3072]{1,0:T(8,128)}) %all-gather.2.cloned.1.call-update) | async-done | bytes 12582928 | tf_op jit(solution)/shard_map/all_gather | solution.py:532
  186.4 3.1 %constant_dynamic-slice_fusion.refs_0_ = f32[1024,512]{1,0:T(8,128)} fusion(f32[1024,3072]{1,0:T(8,128)} %all-gather.2.cloned.1.call-done.square_ref.left_ref, s32[]{:T(128)S(6)} %select_n.239), kind=kLoop, calls=%fused_computation.32 | loop fusion | bytes 4194308 | tf_op jit(solution)/shard_map/dynamic_slice | solution.py:540
  189.5 2.0 collective-permute-start.15
  191.5 2.0 collective-permute-start.14
  193.4 1.3 collective-permute-start.13
  194.8 1.0 copy-done.3
  195.8 9.9 %all-to-all-start.2 = ((f32[16,96,512]{2,1,0:T(8,128)}), f32[16,96,512]{2,1,0:T(8,128)S(1)}, u32[]{:S(2)}, u32[]{:S(2)}) async-start(f32[16,96,512]{2,1,0:T(8,128)} %widen.3), calls=%async_computation.2 | async-start | bytes 6291456 | tf_op jit(solution)/shard_map/all_to_all | solution.py:448
  205.7 61.4 %inverse_factor.1 = (bf16[1024,1024]{1,0:T(8,128)(2,1)S(1)}, bf16[1024,1024]{1,0:T(8,128)(2,1)S(1)}) custom-call(f32[1024,3072]{1,0:T(8,128)} %all-gather.2.cloned.1.call-done.square_ref.left_ref), custom_call_target="tpu_custom_call" | custom-call | flops 65000001536 | bytes 8388608 | tf_op jit(solution)/shard_map/inverse_factor/pallas_call | solution.py:284
  267.1 16.7 %finish.1.part_ref = f32[2048,512]{1,0:T(8,128)} custom-call(s32[2]{0:T(128)S(1)} %copy-done.6, f32[2048,512]{1,0:T(8,128)S(1)} %bitcast.98, f32[1024,3072]{1,0:T(8,128)} %all-gather.2.cloned.1.call-done.square_ref.left_ref, bf16[1024,1024]{1,0:T(8,128)(2,1)S(1)} %get-tuple-element.17.inv_high_ref, bf16[1024,1024]{1,0:T(8,128)(2,1)S(1)} %get-tuple-element.18.inv_low_ref, ...), custom_call_target="tpu_custom_call" | custom-call | flops 16000000000 | bytes 27262976 | tf_op jit(solution)/shard_map/finish/pallas_call | solution.py:379
  283.9 1.2 copy-done.4
  285.1 5.4 %land.1 = f32[2048,512]{1,0:T(8,128)} custom-call(s32[2,16]{1,0:T(2,128)S(1)} %copy-done.5, s32[2]{0:T(128)S(1)} %copy-done.6, f32[2048,512]{1,0:T(8,128)} %finish.1.part_ref, f32[16,32,512]{2,1,0:T(8,128)S(1)} %copy-done.4, f32[16,96,512]{2,1,0:T(8,128)S(1)} %all-to-all-done.2.late_ref), custom_call_target="tpu_custom_call", output_to_operand_aliasing={{}: (2, {})} | custom-call | flops 5000000000 | bytes 12582912 | tf_op jit(solution)/shard_map/land/pallas_call | solution.py:428
  (48 shorter events, 2.3 us)
Async XLA Ops:
  8.1 1.6 copy-start
  14.2 25.4 %copy-start.9 = (s32[4,2]{0,1:T(2,128)S(1)}, s32[4,2]{0,1:T(2,128)}, u32[]{:S(2)}) copy-start(s32[4,2]{0,1:T(2,128)} %param.7) | copy-start | bytes 100
  14.2 28.7 %copy-start.1 = (f32[1,2,64,4096]{3,2,1,0:T(8,128)S(1)}, f32[1,2,64,4096]{3,2,1,0:T(8,128)}, u32[]{:S(2)}) copy-start(f32[1,2,64,4096]{3,2,1,0:T(8,128)} %param.5) | copy-start | bytes 6291460
  14.2 29.8 %all-to-all-start = ((f32[16,2,32,128]{3,2,1,0:T(8,128)}), f32[16,2,32,128]{3,2,1,0:T(8,128)}, u32[]{:S(2)}, u32[]{:S(2)}) async-start(f32[16,2,32,128]{3,2,1,0:T(8,128)} %pick.1), calls=%async_computation | async-start | bytes 1048576 | tf_op jit(solution)/shard_map/all_to_all | solution.py:448
  22.3 164.1 %all-gather.2.cloned.1.call-start = ((), (), s32[]{:S(2)}) async-start(), calls=%async_computation.3 | async-start | bytes 13369344 | tf_op jit(solution)/shard_map/all_gather | solution.py:532
  24.5 26.6 %collective-permute-start.6 = (f32[64,512]{1,0:T(8,128)}, f32[64,512]{1,0:T(8,128)}, u32[]{:S(2)}, u32[]{:S(2)}) collective-permute-start(f32[64,512]{1,0:T(8,128)} %get-tuple-element.27), channel_id=1, source_target_pairs={{0,12},{1,28},{2,44},{3,60},{4,0},{5,16},{6,32},{7,48},{8,4},{9,20... | collective-permute-start | bytes 393224 | tf_op jit(solution)/shard_map/ppermute | solution.py:468
  29.2 23.8 %collective-permute-start.4 = (f32[64,512]{1,0:T(8,128)}, f32[64,512]{1,0:T(8,128)}, u32[]{:S(2)}, u32[]{:S(2)}) collective-permute-start(f32[64,512]{1,0:T(8,128)} %get-tuple-element.28), channel_id=1, source_target_pairs={{0,8},{1,24},{2,40},{3,56},{4,12},{5,28},{6,44},{7,60},{8,0},{9,16... | collective-permute-start | bytes 393224 | tf_op jit(solution)/shard_map/ppermute | solution.py:468
  33.0 21.9 %collective-permute-start.2 = (f32[64,512]{1,0:T(8,128)}, f32[64,512]{1,0:T(8,128)}, u32[]{:S(2)}, u32[]{:S(2)}) collective-permute-start(f32[64,512]{1,0:T(8,128)} %get-tuple-element.29), channel_id=1, source_target_pairs={{0,4},{1,20},{2,36},{3,52},{4,8},{5,24},{6,40},{7,56},{8,12},{9,28... | collective-permute-start | bytes 393224 | tf_op jit(solution)/shard_map/ppermute | solution.py:468
  35.0 21.9 %collective-permute-start.1 = (f32[64,512]{1,0:T(8,128)S(1)}, f32[64,512]{1,0:T(8,128)}, u32[]{:S(2)}, u32[]{:S(2)}) collective-permute-start(f32[64,512]{1,0:T(8,128)S(1)} %get-tuple-element.30), channel_id=1, source_target_pairs={{0,2},{1,18},{2,34},{3,50},{4,6},{5,22},{6,38},{7,54},{8,10},{9,26... | collective-permute-start | bytes 393224 | tf_op jit(solution)/shard_map/ppermute | solution.py:468
  45.7 26.0 %collective-permute-start.8 = (f32[16,32,128]{2,1,0:T(8,128)S(1)}, f32[16,32,128]{2,1,0:T(8,128)S(1)}, u32[]{:S(2)}, u32[]{:S(2)}) collective-permute-start(f32[16,32,128]{2,1,0:T(8,128)S(1)} %get-tuple-element.33), channel_id=1, source_target_pairs={{0,64},{64,0},{128,192},{192,128},{1,65},{65,1},{129,193},{193,129... | collective-permute-start | bytes 786440 | tf_op jit(solution)/shard_map/ppermute | solution.py:522
  46.9 4.2 %copy-start.8 = (f32[64,512]{1,0:T(8,128)S(1)}, f32[64,512]{1,0:T(8,128)}, u32[]{:S(2)}) copy-start(f32[64,512]{1,0:T(8,128)} %get-tuple-element.23) | copy-start | bytes 393220
  46.9 6.1 %copy-start.7 = (f32[64,512]{1,0:T(8,128)S(1)}, f32[64,512]{1,0:T(8,128)}, u32[]{:S(2)}) copy-start(f32[64,512]{1,0:T(8,128)} %get-tuple-element.24) | copy-start | bytes 393220
  51.1 16.2 %collective-permute-start.7 = (f32[64,512]{1,0:T(8,128)S(1)}, f32[64,512]{1,0:T(8,128)S(1)}, u32[]{:S(2)}, u32[]{:S(2)}) collective-permute-start(f32[64,512]{1,0:T(8,128)S(1)} %copy-done.8), channel_id=1, source_target_pairs={{0,14},{1,30},{2,46},{3,62},{4,2},{5,18},{6,34},{7,50},{8,6},{9,22... | collective-permute-start | bytes 393224 | tf_op jit(solution)/shard_map/ppermute | solution.py:468
  53.0 18.7 %collective-permute-start.5 = (f32[64,512]{1,0:T(8,128)S(1)}, f32[64,512]{1,0:T(8,128)S(1)}, u32[]{:S(2)}, u32[]{:S(2)}) collective-permute-start(f32[64,512]{1,0:T(8,128)S(1)} %copy-done.7), channel_id=1, source_target_pairs={{0,10},{1,26},{2,42},{3,58},{4,14},{5,30},{6,46},{7,62},{8,2},{9,1... | collective-permute-start | bytes 393224 | tf_op jit(solution)/shard_map/ppermute | solution.py:468
  55.0 16.8 %collective-permute-start.3 = (f32[64,512]{1,0:T(8,128)S(1)}, f32[64,512]{1,0:T(8,128)S(1)}, u32[]{:S(2)}, u32[]{:S(2)}) collective-permute-start(f32[64,512]{1,0:T(8,128)S(1)} %get-tuple-element.25), channel_id=1, source_target_pairs={{0,6},{1,22},{2,38},{3,54},{4,10},{5,26},{6,42},{7,58},{8,14},{9,3... | collective-permute-start | bytes 393224 | tf_op jit(solution)/shard_map/ppermute | solution.py:468
  56.9 14.9 %collective-permute-start = (f32[64,512]{1,0:T(8,128)S(1)}, f32[64,512]{1,0:T(8,128)S(1)}, u32[]{:S(2)}, u32[]{:S(2)}) collective-permute-start(f32[64,512]{1,0:T(8,128)S(1)} %get-tuple-element.26), channel_id=1, source_target_pairs={{0,0},{1,16},{2,32},{3,48},{4,4},{5,20},{6,36},{7,52},{8,8},{9,24}... | collective-permute-start | bytes 393224 | tf_op jit(solution)/shard_map/ppermute | solution.py:468
  67.3 4.5 %copy-start.11 = (f32[64,512]{1,0:T(8,128)}, f32[64,512]{1,0:T(8,128)S(1)}, u32[]{:S(2)}) copy-start(f32[64,512]{1,0:T(8,128)S(1)} %collective-permute-done.7.refs_7_) | copy-start | bytes 393220
  71.7 0.7 copy-start.12
  71.7 0.7 copy-start.13
  71.8 0.7 copy-start.14
  71.8 0.8 copy-start.10
  75.7 5.7 %collective-permute-start.11 = (f32[64,512]{1,0:T(8,128)}, f32[64,512]{1,0:T(8,128)S(1)}, u32[]{:S(2)}, u32[]{:S(2)}) collective-permute-start(f32[64,512]{1,0:T(8,128)} %get-tuple-element.15), channel_id=1, source_target_pairs={{0,16},{16,32},{1,17},{17,33},{2,18},{18,34},{3,19},{19,35},{4,20}... | collective-permute-start | bytes 393224 | tf_op jit(solution)/shard_map/ppermute | solution.py:489
  78.0 4.1 %collective-permute-start.10 = (f32[64,512]{1,0:T(8,128)}, f32[64,512]{1,0:T(8,128)S(1)}, u32[]{:S(2)}, u32[]{:S(2)}) collective-permute-start(f32[64,512]{1,0:T(8,128)} %get-tuple-element.15), channel_id=1, source_target_pairs={{0,32},{16,48},{1,33},{17,49},{2,34},{18,50},{3,35},{19,51},{4,36}... | collective-permute-start | bytes 393224 | tf_op jit(solution)/shard_map/ppermute | solution.py:489
  79.3 5.9 %collective-permute-start.9 = (f32[64,512]{1,0:T(8,128)}, f32[64,512]{1,0:T(8,128)S(1)}, u32[]{:S(2)}, u32[]{:S(2)}) collective-permute-start(f32[64,512]{1,0:T(8,128)} %get-tuple-element.15), channel_id=1, source_target_pairs={{0,48},{16,0},{1,49},{17,1},{2,50},{18,2},{3,51},{19,3},{4,52},{20... | collective-permute-start | bytes 393224 | tf_op jit(solution)/shard_map/ppermute | solution.py:489
  88.5 106.2 %all-to-all-start.1 = ((f32[16,32,512]{2,1,0:T(8,128)}), f32[16,32,512]{2,1,0:T(8,128)S(1)}, u32[]{:S(2)}, u32[]{:S(2)}) async-start(f32[16,32,512]{2,1,0:T(8,128)} %widen.2), calls=%async_computation.1 | async-start | bytes 2097152 | tf_op jit(solution)/shard_map/all_to_all | solution.py:448
  99.3 24.7 %collective-permute-start.12 = (f32[64,4096]{1,0:T(8,128)}, f32[64,4096]{1,0:T(8,128)S(1)}, u32[]{:S(2)}, u32[]{:S(2)}) collective-permute-start(f32[64,4096]{1,0:T(8,128)} %get-tuple-element.31), channel_id=1, source_target_pairs={{0,64},{64,0},{128,192},{192,128},{1,65},{65,1},{129,193},{193,129... | collective-permute-start | bytes 3145736 | tf_op jit(solution)/shard_map/ppermute | solution.py:534
  189.5 77.6 %collective-permute-start.15 = (f32[1024,512]{1,0:T(8,128)}, f32[1024,512]{1,0:T(8,128)}, u32[]{:S(2)}, u32[]{:S(2)}) collective-permute-start(f32[1024,512]{1,0:T(8,128)} %constant_dynamic-slice_fusion.refs_0_), channel_id=1, source_target_pairs={{0,48},{17,1},{34,18},{51,35},{4,52},{21,5},{38,22},{55,39},{8,56}... | collective-permute-start | bytes 6291464 | tf_op jit(solution)/shard_map/ppermute | solution.py:479
  191.5 75.6 %collective-permute-start.14 = (f32[1024,512]{1,0:T(8,128)}, f32[1024,512]{1,0:T(8,128)}, u32[]{:S(2)}, u32[]{:S(2)}) collective-permute-start(f32[1024,512]{1,0:T(8,128)} %constant_dynamic-slice_fusion.refs_0_), channel_id=1, source_target_pairs={{0,32},{17,49},{34,2},{51,19},{4,36},{21,53},{38,6},{55,23},{8,40}... | collective-permute-start | bytes 6291464 | tf_op jit(solution)/shard_map/ppermute | solution.py:479
  193.4 73.7 %collective-permute-start.13 = (f32[1024,512]{1,0:T(8,128)}, f32[1024,512]{1,0:T(8,128)}, u32[]{:S(2)}, u32[]{:S(2)}) collective-permute-start(f32[1024,512]{1,0:T(8,128)} %constant_dynamic-slice_fusion.refs_0_), channel_id=1, source_target_pairs={{0,16},{17,33},{34,50},{51,3},{4,20},{21,37},{38,54},{55,7},{8,24}... | collective-permute-start | bytes 6291464 | tf_op jit(solution)/shard_map/ppermute | solution.py:479
  194.7 1.0 copy-start.3
  195.8 88.1 %all-to-all-start.2 = ((f32[16,96,512]{2,1,0:T(8,128)}), f32[16,96,512]{2,1,0:T(8,128)S(1)}, u32[]{:S(2)}, u32[]{:S(2)}) async-start(f32[16,96,512]{2,1,0:T(8,128)} %widen.3), calls=%async_computation.2 | async-start | bytes 6291456 | tf_op jit(solution)/shard_map/all_to_all | solution.py:448
  205.7 61.4 %copy-start.2 = (f32[1,2048,512]{2,1,0:T(8,128)S(1)}, f32[1,2048,512]{2,1,0:T(8,128)}, u32[]{:S(2)}) copy-start(f32[1,2048,512]{2,1,0:T(8,128)} %param.4) | copy-start | bytes 12582916
  205.7 61.4 %copy-start.6 = (s32[2]{0:T(128)S(1)}, s32[2]{0:T(128)}, u32[]{:S(2)}) copy-start(s32[2]{0:T(128)} %pad_add_fusion.1.place_ref) | copy-start | bytes 28
  267.1 16.7 %copy-start.5 = (s32[2,16]{1,0:T(2,128)S(1)}, s32[2,16]{1,0:T(2,128)}, u32[]{:S(2)}) copy-start(s32[2,16]{1,0:T(2,128)} %constant_dynamic-slice_fusion.2.target_ref) | copy-start | bytes 388
  283.9 1.2 copy-start.4
Sparse Core Ops, SparseCore 0:
  88.7 97.6 all-gather.1
